TPU v7x, 128 devices: a whole 4x4x4 slice. The times are simulated.
128 devices in a mesh: grid: 4 (over y_hi, core), tile: 32 (over y_lo, x, z).
Axes of the slice: x: 4, y: 4 (y_hi: 2, y_lo: 2; y = y_hi * 2 + y_lo), z: 4, core: 2. Of those that a mesh axis runs over, the one named last changes fastest.
Arguments:
- state_field: float32 [4, 512, 4, 4, 4, 4, 128], P('grid', 'tile'), may hold values from -6 to 6
- levels: int32 [4, 6], P('grid'), may hold values from 1 to 4
- sign_bits: int32 [4], P('grid'), may hold values from 0 to 1
Outputs:
- combined_field: float32 [4, 512, 4, 4, 4, 4, 128], P('grid', 'tile')
All inputs are finite; a program needn't handle non-finite values.
Results may differ from a plain program's by a relative error of at most 0.0003.
Values sent between devices are 32-bit elements; how exact they have to be, the bound alone decides.
No kernel may reach another device: no remote copies, remote signals or barrier semaphores. Data moves between devices by JAX's collectives and lax.ppermute only.
A program may use at most 64 MiB of HBM per device.

v0:
```python
import jax
import jax.numpy as jnp
from jax import lax
from jax.experimental import pallas as pl
from jax.experimental.pallas import tpu as pltpu
from jax.sharding import PartitionSpec as P

SCALE = 6.4
ROWS = 32
HALF = ROWS // 2


def devices_of(mesh):
    return mesh.shape["grid"], mesh.shape["tile"]


def layer_update(read_f, read_g, read_v, coef, masks, own, other, emit):
    low, first, last = masks
    centre, rate = coef
    for d2 in range(2):
        for d3 in range(4):
            rows = [own + d2 * 8 + d3 * 2 + a for a in range(2)]
            up2 = [(own + 8 if d2 == 0 else other) + d3 * 2 + a for a in range(2)]
            down2 = [(other + 8 if d2 == 0 else own) + d3 * 2 + a for a in range(2)]
            up3 = [own + d2 * 8 + (d3 + 1) % 4 * 2 + a for a in range(2)]
            down3 = [own + d2 * 8 + (d3 + 3) % 4 * 2 + a for a in range(2)]
            f = [read_f(0, row) for row in rows]
            g = [read_g(0, row) for row in rows]
            turned = [pltpu.roll(f[a] + g[1 - a], 4, 0) for a in range(2)]
            for a in range(2):
                total = centre * read_v(0, rows[a])
                total += rate[0] * (read_f(1, rows[a]) + read_g(-1, rows[a]))
                total += rate[1] * (read_f(0, up2[a]) + read_g(0, down2[a]))
                total += rate[2] * (read_f(0, up3[a]) + read_g(0, down3[a]))
                total += rate[3] * jnp.where(low, turned[a], turned[1 - a])
                ahead = jnp.where(last, pltpu.roll(f[a], 3, 0), pltpu.roll(f[a], 7, 0))
                behind = jnp.where(first, pltpu.roll(g[a], 5, 0), pltpu.roll(g[a], 1, 0))
                total += rate[4] * (ahead + behind)
                total += rate[5] * (pltpu.roll(f[a], 127, 1) + pltpu.roll(g[a], 1, 1))
                emit(d2 * 8 + d3 * 2 + a, rows[a], total)


def lane_masks():
    sub = lax.broadcasted_iota(jnp.int32, (8, 128), 0)
    return sub < 4, sub % 4 == 0, sub % 4 == 3


def coefficients(rates_ref):
    rate = [0.08 * rates_ref[d] for d in range(6)]
    total = rate[0] + rate[1] + rate[2] + rate[3] + rate[4] + rate[5]
    return 1.0 - 2.0 * total, rate


def put(vs, fs, gs, slot, layer, row, v):
    q = v * v
    vs[slot, layer, row] = v
    fs[slot, layer, row] = v - q
    gs[slot, layer, row] = v + q


def load_layer(vs, fs, gs, slot, layer, source, index, scale):
    for row in range(ROWS):
        v = source[index, row]
        put(vs, fs, gs, slot, layer, row, v * scale if scale is not None else v)


def step_layer(vs, fs, gs, slot, layer, coef, masks):
    for half in range(2):
        layer_update(
            lambda dx, row: fs[slot, layer + dx, row],
            lambda dx, row: gs[slot, layer + dx, row],
            lambda dx, row: vs[slot, layer + dx, row],
            coef, masks, half * HALF, (1 - half) * HALF,
            lambda at, row, v: put(vs, fs, gs, 1 - slot, layer, row, v),
        )


def last_layer(vs, fs, gs, slot, layer, coef, masks, core, sign, keep, send, out):
    for part, ref in ((0, keep), (1, send)):
        own = (core ^ part) * HALF

        def emit(at, row, v, ref=ref):
            ref[out, at] = v * sign

        layer_update(
            lambda dx, row: fs[slot, layer + dx, row],
            lambda dx, row: gs[slot, layer + dx, row],
            lambda dx, row: vs[slot, layer + dx, row],
            coef, masks, own, HALF - own, emit,
        )


def loop(low, high, body):
    lax.fori_loop(low, high, lambda i, carry: (body(i), carry)[1], 0)


def middle_kernel(rates, scalars, u, keep, send, edge_l, edge_r, vs, fs, gs):
    coef, masks = coefficients(rates), lane_masks()
    loop(0, 16, lambda i: load_layer(vs, fs, gs, 0, i, u, i, 1.0 / SCALE))
    for step in range(1, 4):
        slot = (step - 1) % 2
        loop(step, 16 - step, lambda i, s=slot: step_layer(vs, fs, gs, s, i, coef, masks))
        for k in range(2):
            edge_l[2 * (step - 1) + k] = vs[1 - slot, step + k]
            edge_r[2 * (step - 1) + k] = vs[1 - slot, 14 - step + k]
    core, sign = scalars[0], (scalars[1] * 2 - 1).astype(jnp.float32) * SCALE
    loop(0, 8, lambda i: last_layer(vs, fs, gs, 1, i + 4, coef, masks, core, sign, keep, send, i))


def outer_kernel(rates, scalars, u, halo_l, halo_r, edge_l, edge_r, keep, send, vs, fs, gs):
    coef, masks = coefficients(rates), lane_masks()
    inv = 1.0 / SCALE
    loop(0, 4, lambda i: load_layer(vs, fs, gs, 0, i, halo_l, i, inv))
    loop(0, 2, lambda i: load_layer(vs, fs, gs, 0, 4 + i, u, i, inv))
    loop(0, 2, lambda i: load_layer(vs, fs, gs, 0, 13 + i, u, 14 + i, inv))
    loop(0, 5, lambda i: load_layer(vs, fs, gs, 0, 15 + i, halo_r, i, inv))
    for step in range(1, 4):
        slot = (step - 1) % 2
        loop(step, step + 4, lambda i, s=slot: step_layer(vs, fs, gs, s, i, coef, masks))
        loop(15 - step, 20 - step, lambda i, s=slot: step_layer(vs, fs, gs, s, i, coef, masks))
        for k in range(2):
            load_layer(vs, fs, gs, 1 - slot, 4 + step + k, edge_l, 2 * (step - 1) + k, None)
            load_layer(vs, fs, gs, 1 - slot, 13 - step + k, edge_r, 2 * (step - 1) + k, None)
    core, sign = scalars[0], (scalars[1] * 2 - 1).astype(jnp.float32) * SCALE
    loop(0, 4, lambda i: last_layer(vs, fs, gs, 1, i + 4, coef, masks, core, sign, keep, send, i))
    loop(0, 5, lambda i: last_layer(vs, fs, gs, 1, i + 11, coef, masks, core, sign, keep, send, i + 4))


def rebuild_kernel(scalars, mid_own, mid_other, out_own, out_other, result, full):
    core, shift = scalars[0], scalars[2]
    spacing = jnp.left_shift(jnp.int32(1), shift)
    for half, mid, outer in ((core, mid_own, out_own), (1 - core, mid_other, out_other)):
        rows = pl.ds(half * HALF, HALF)

        def place(i, half=half, mid=mid, outer=outer, rows=rows):
            full[4 + i, rows] = mid[i]

        loop(0, 8, place)
        for i in range(4):
            full[i, rows] = outer[i]
        for i in range(5):
            full[12 + i, rows] = outer[4 + i]

    def one(i):
        anchor = jnp.left_shift(jnp.right_shift(i, shift), shift)
        right = (i - anchor).astype(jnp.float32) / spacing.astype(jnp.float32)
        result[i] = full[anchor] * (1.0 - right) + full[anchor + spacing] * right

    loop(0, 16, one)


VMEM = pl.BlockSpec(memory_space=pltpu.VMEM)
SMEM = pl.BlockSpec(memory_space=pltpu.SMEM)
F32 = jnp.float32


def shape(*dims):
    return jax.ShapeDtypeStruct(dims, F32)


def call(kernel, name, n_smem, n_in, outs, scratch, layers):
    work = layers * ROWS * 8 * 128
    return pl.pallas_call(
        kernel,
        name=name,
        out_shape=outs,
        in_specs=[SMEM] * n_smem + [VMEM] * n_in,
        out_specs=jax.tree.map(lambda _: VMEM, outs),
        scratch_shapes=scratch,
        cost_estimate=pl.CostEstimate(flops=work * 40, bytes_accessed=work * 8, transcendentals=0),
        compiler_params=pltpu.CompilerParams(vmem_limit_bytes=48 << 20),
    )


def on_device(grids, tiles, state_field, levels, sign_bits):
    u = state_field.reshape(16, ROWS, 8, 128)

    def flat(y, core, rest):
        return ((y // 2) * 2 + core) * tiles + (y % 2) * (tiles // 2) + rest

    every = [(y, c, r) for y in range(grids) for c in range(2) for r in range(tiles // 2)]
    to_core = [(flat(y, c, r), flat(y, 1 - c, r)) for y, c, r in every]
    to_far = [(flat(y, c, r), flat((y + 2) % 4, c, r)) for y, c, r in every]

    def send(x, pairs):
        return lax.ppermute(x, ("grid", "tile"), pairs)

    halo_l = lax.ppermute(u[12:], "tile", [(i, (i + 1) % tiles) for i in range(tiles)])
    halo_r = lax.ppermute(u[:5], "tile", [((i + 1) % tiles, i) for i in range(tiles)])

    rates = jnp.exp2(levels[0].astype(F32) - 4.0)
    core = lax.axis_index("grid") % 2
    scalars = jnp.stack([core.astype(jnp.int32), sign_bits[0], 4 - levels[0, 0]])

    def buffers(n):
        return [pltpu.VMEM((2, n, ROWS, 8, 128), F32)] * 3

    keep_m, send_m, edge_l, edge_r = call(
        middle_kernel, "middle", 2, 1,
        (shape(8, HALF, 8, 128), shape(8, HALF, 8, 128), shape(6, ROWS, 8, 128), shape(6, ROWS, 8, 128)),
        buffers(16), 44,
    )(rates, scalars, u)
    part_m = keep_m + send(send_m, to_core)
    far_m = send(part_m, to_far)
    keep_o, send_o = call(
        outer_kernel, "outer", 2, 5, (shape(9, HALF, 8, 128), shape(9, HALF, 8, 128)), buffers(20), 36,
    )(rates, scalars, u, halo_l, halo_r, edge_l, edge_r)
    part_o = keep_o + send(send_o, to_core)
    far_o = send(part_o, to_far)
    own_m = part_m + far_m
    other_m = send(own_m, to_core)
    own_o = part_o + far_o
    other_o = send(own_o, to_core)
    result = call(
        rebuild_kernel, "rebuild", 1, 4, shape(16, ROWS, 8, 128), [pltpu.VMEM((17, ROWS, 8, 128), F32)], 2,
    )(scalars, own_m, other_m, own_o, other_o)
    return result.reshape(state_field.shape)


def solution(mesh):
    grids, tiles = devices_of(mesh)
    placed = (P("grid", "tile", None, None, None, None, None), P("grid", None), P("grid"))
    return jax.shard_map(
        lambda *args: on_device(grids, tiles, *args),
        mesh=mesh,
        in_specs=placed,
        out_specs=P("grid", "tile", None, None, None, None, None),
        check_vma=False,
    )
```

profile of v0, /device:TPU:1, one launch (start us, length us, event | category | flops | bytes accessed | tf_op | source)
XLA Modules:
  0.0 72.5 jit_solution(14357747342472524779)
XLA Ops:
  0.0 0.0 copy-start
  0.0 0.0 copy-start.1
  0.0 2.1 %slice.18 = f32[1,5,4,4,4,4,128]{6,5,4,3,2,1,0:T(4,128)} slice(f32[1,16,4,4,4,4,128]{6,5,4,3,2,1,0:T(4,128)} %param.3), slice={[0:1], [0:5], [0:4], [0:4], [0:4], [0:4], [0:128]} | slice | bytes 1310720 | tf_op jit(solution)/shard_map/slice | solution.py:189
  2.2 7.8 %collective-permute-start.4 = (f32[5,32,8,128]{3,2,1,0:T(8,128)}, f32[5,32,8,128]{3,2,1,0:T(8,128)S(1)}, u32[]{:S(2)}, u32[]{:S(2)}) collective-permute-start(f32[5,32,8,128]{3,2,1,0:T(8,128)} %bitcast.5), channel_id=1, source_target_pairs={{1,0},{2,1},{3,2},{4,3},{5,4},{6,5},{7,6},{8,7},{9,8},{10,9},{11,1... | collective-permute-start | bytes 1966088 | tf_op jit(solution)/shard_map/ppermute | solution.py:189
  9.9 1.9 %slice.16 = f32[1,4,4,4,4,4,128]{6,5,4,3,2,1,0:T(4,128)} slice(f32[1,16,4,4,4,4,128]{6,5,4,3,2,1,0:T(4,128)} %param.3), slice={[0:1], [12:16], [0:4], [0:4], [0:4], [0:4], [0:128]} | slice | bytes 1048576 | tf_op jit(solution)/shard_map/slice | solution.py:188
  11.8 0.0 collective-permute-start.3
  12.5 0.0 copy-done.1
  12.5 0.1 pad_add_fusion.scalars
  12.6 0.0 copy-done
  12.6 7.8 %middle.1 = (f32[8,16,8,128]{3,2,1,0:T(8,128)S(1)}, f32[8,16,8,128]{3,2,1,0:T(8,128)S(1)}, f32[6,32,8,128]{3,2,1,0:T(8,128)S(1)}, f32[6,32,8,128]{3,2,1,0:T(8,128)S(1)}) custom-call(f32[6]{0:T(128)S(1)} %exponential_bitcast_fusion.rates, s32[3]{0:T(128)S(1)} %pad_add_fusion.scalars, f32[16,32,8,128]{3,2,1,0:T(8,128)S(1)} %bitcast.9), custom_call_target="tpu_custom_call" | custom-call | flops 57671680 | bytes 11534336 | tf_op jit(solution)/shard_map/middle/pallas_call | solution.py:198
  20.4 8.3 %collective-permute-done.3.halo_l = f32[4,32,8,128]{3,2,1,0:T(8,128)S(1)} collective-permute-done((f32[4,32,8,128]{3,2,1,0:T(8,128)}, f32[4,32,8,128]{3,2,1,0:T(8,128)S(1)}, u32[]{:S(2)}, u32[]{:S(2)}) %collective-permute-start.3) | collective-permute-done | bytes 524320 | tf_op jit(solution)/shard_map/ppermute | solution.py:188
  28.7 0.0 collective-permute-done.4.halo_r
  28.7 6.8 %outer.1 = (f32[9,16,8,128]{3,2,1,0:T(8,128)S(1)}, f32[9,16,8,128]{3,2,1,0:T(8,128)S(1)}) custom-call(f32[6]{0:T(128)S(1)} %exponential_bitcast_fusion.rates, s32[3]{0:T(128)S(1)} %pad_add_fusion.scalars, f32[16,32,8,128]{3,2,1,0:T(8,128)S(1)} %bitcast.10, f32[4,32,8,128]{3,2,1,0:T(8,128)S(1)} %collective-permute-done.3.halo_l, ...), custom_call_target="tpu_custom_call" | custom-call | flops 47185920 | bytes 9437184 | tf_op jit(solution)/shard_map/outer/pallas_call | solution.py:205
  35.6 1.9 %collective-permute-start.5 = (f32[9,16,8,128]{3,2,1,0:T(8,128)S(1)}, f32[9,16,8,128]{3,2,1,0:T(8,128)S(1)}, u32[]{:S(2)}, u32[]{:S(2)}) collective-permute-start(f32[9,16,8,128]{3,2,1,0:T(8,128)S(1)} %get-tuple-element.16), channel_id=1, source_target_pairs={{0,32},{1,33},{2,34},{3,35},{4,36},{5,37},{6,38},{7,39},{8,40},{9,... | collective-permute-start | bytes 1769480 | tf_op jit(solution)/shard_map/ppermute | solution.py:186
  37.5 0.1 collective-permute-start
  37.6 1.5 %collective-permute-done.5 = f32[9,16,8,128]{3,2,1,0:T(8,128)S(1)} collective-permute-done((f32[9,16,8,128]{3,2,1,0:T(8,128)S(1)}, f32[9,16,8,128]{3,2,1,0:T(8,128)S(1)}, u32[]{:S(2)}, u32[]{:S(2)}) %collective-permute-start.5) | collective-permute-done | bytes 589856 | tf_op jit(solution)/shard_map/ppermute | solution.py:186
  39.1 0.1 add.21
  39.2 2.7 %collective-permute-start.6 = (f32[9,16,8,128]{3,2,1,0:T(8,128)S(1)}, f32[9,16,8,128]{3,2,1,0:T(8,128)S(1)}, u32[]{:S(2)}, u32[]{:S(2)}) collective-permute-start(f32[9,16,8,128]{3,2,1,0:T(8,128)S(1)} %add.21), channel_id=1, source_target_pairs={{0,64},{1,65},{2,66},{3,67},{4,68},{5,69},{6,70},{7,71},{8,72},{9,... | collective-permute-start | bytes 1769480 | tf_op jit(solution)/shard_map/ppermute | solution.py:186
  41.9 0.0 collective-permute-done
  41.9 0.1 add.19
  42.0 0.7 collective-permute-start.1
  42.7 12.7 %collective-permute-done.6 = f32[9,16,8,128]{3,2,1,0:T(8,128)S(1)} collective-permute-done((f32[9,16,8,128]{3,2,1,0:T(8,128)S(1)}, f32[9,16,8,128]{3,2,1,0:T(8,128)S(1)}, u32[]{:S(2)}, u32[]{:S(2)}) %collective-permute-start.6) | collective-permute-done | bytes 589856 | tf_op jit(solution)/shard_map/ppermute | solution.py:186
  55.4 0.1 add.22.out_own
  55.4 2.1 %collective-permute-start.7 = (f32[9,16,8,128]{3,2,1,0:T(8,128)S(1)}, f32[9,16,8,128]{3,2,1,0:T(8,128)S(1)}, u32[]{:S(2)}, u32[]{:S(2)}) collective-permute-start(f32[9,16,8,128]{3,2,1,0:T(8,128)S(1)} %add.22.out_own), channel_id=1, source_target_pairs={{0,32},{1,33},{2,34},{3,35},{4,36},{5,37},{6,38},{7,39},{8,40},{9,... | collective-permute-start | bytes 1769480 | tf_op jit(solution)/shard_map/ppermute | solution.py:186
  57.5 9.1 %collective-permute-done.1 = f32[8,16,8,128]{3,2,1,0:T(8,128)S(1)} collective-permute-done((f32[8,16,8,128]{3,2,1,0:T(8,128)S(1)}, f32[8,16,8,128]{3,2,1,0:T(8,128)S(1)}, u32[]{:S(2)}, u32[]{:S(2)}) %collective-permute-start.1) | collective-permute-done | bytes 524320 | tf_op jit(solution)/shard_map/ppermute | solution.py:186
  66.6 0.1 add.20.mid_own
  66.7 1.3 %collective-permute-start.2 = (f32[8,16,8,128]{3,2,1,0:T(8,128)S(1)}, f32[8,16,8,128]{3,2,1,0:T(8,128)S(1)}, u32[]{:S(2)}, u32[]{:S(2)}) collective-permute-start(f32[8,16,8,128]{3,2,1,0:T(8,128)S(1)} %add.20.mid_own), channel_id=1, source_target_pairs={{0,32},{1,33},{2,34},{3,35},{4,36},{5,37},{6,38},{7,39},{8,40},{9,... | collective-permute-start | bytes 1572872 | tf_op jit(solution)/shard_map/ppermute | solution.py:186
  68.0 1.5 %collective-permute-done.2.mid_other = f32[8,16,8,128]{3,2,1,0:T(8,128)S(1)} collective-permute-done((f32[8,16,8,128]{3,2,1,0:T(8,128)S(1)}, f32[8,16,8,128]{3,2,1,0:T(8,128)S(1)}, u32[]{:S(2)}, u32[]{:S(2)}) %collective-permute-start.2) | collective-permute-done | bytes 524320 | tf_op jit(solution)/shard_map/ppermute | solution.py:186
  69.5 0.0 collective-permute-done.7.out_other
  69.5 3.0 %rebuild.1 = f32[16,32,8,128]{3,2,1,0:T(8,128)} custom-call(s32[3]{0:T(128)S(1)} %pad_add_fusion.scalars, f32[8,16,8,128]{3,2,1,0:T(8,128)S(1)} %add.20.mid_own, f32[8,16,8,128]{3,2,1,0:T(8,128)S(1)} %collective-permute-done.2.mid_other, f32[9,16,8,128]{3,2,1,0:T(8,128)S(1)} %add.22.out_own, f32[9,16,8,128]{3,2,1,0:T(8,128)S(1)} %collective-permute-done.7.out_other), custom_call_target="tpu_custom_call" | custom-call | flops 2621440 | bytes 524288 | tf_op jit(solution)/shard_map/rebuild/pallas_call | solution.py:214
  (1 shorter events, 0.0 us)
Async XLA Ops:
  0.0 12.6 %copy-start = (f32[1,16,4,4,4,4,128]{6,5,4,3,2,1,0:T(4,128)S(1)}, f32[1,16,4,4,4,4,128]{6,5,4,3,2,1,0:T(4,128)}, u32[]{:S(2)}) copy-start(f32[1,16,4,4,4,4,128]{6,5,4,3,2,1,0:T(4,128)} %param.3) | copy-start | bytes 6291460
  0.0 12.5 %copy-start.1 = (s32[1,6]{1,0:T(1,128)S(1)}, s32[1,6]{1,0:T(1,128)}, u32[]{:S(2)}) copy-start(s32[1,6]{1,0:T(1,128)} %param.4) | copy-start | bytes 76
  2.2 26.6 %collective-permute-start.4 = (f32[5,32,8,128]{3,2,1,0:T(8,128)}, f32[5,32,8,128]{3,2,1,0:T(8,128)S(1)}, u32[]{:S(2)}, u32[]{:S(2)}) collective-permute-start(f32[5,32,8,128]{3,2,1,0:T(8,128)} %bitcast.5), channel_id=1, source_target_pairs={{1,0},{2,1},{3,2},{4,3},{5,4},{6,5},{7,6},{8,7},{9,8},{10,9},{11,1... | collective-permute-start | bytes 1966088 | tf_op jit(solution)/shard_map/ppermute | solution.py:189
  11.8 16.9 %collective-permute-start.3 = (f32[4,32,8,128]{3,2,1,0:T(8,128)}, f32[4,32,8,128]{3,2,1,0:T(8,128)S(1)}, u32[]{:S(2)}, u32[]{:S(2)}) collective-permute-start(f32[4,32,8,128]{3,2,1,0:T(8,128)} %bitcast.4), channel_id=1, source_target_pairs={{0,1},{1,2},{2,3},{3,4},{4,5},{5,6},{6,7},{7,8},{8,9},{9,10},{10,1... | collective-permute-start | bytes 1572872 | tf_op jit(solution)/shard_map/ppermute | solution.py:188
  35.6 3.6 %collective-permute-start.5 = (f32[9,16,8,128]{3,2,1,0:T(8,128)S(1)}, f32[9,16,8,128]{3,2,1,0:T(8,128)S(1)}, u32[]{:S(2)}, u32[]{:S(2)}) collective-permute-start(f32[9,16,8,128]{3,2,1,0:T(8,128)S(1)} %get-tuple-element.16), channel_id=1, source_target_pairs={{0,32},{1,33},{2,34},{3,35},{4,36},{5,37},{6,38},{7,39},{8,40},{9,... | collective-permute-start | bytes 1769480 | tf_op jit(solution)/shard_map/ppermute | solution.py:186
  37.5 4.4 %collective-permute-start = (f32[8,16,8,128]{3,2,1,0:T(8,128)S(1)}, f32[8,16,8,128]{3,2,1,0:T(8,128)S(1)}, u32[]{:S(2)}, u32[]{:S(2)}) collective-permute-start(f32[8,16,8,128]{3,2,1,0:T(8,128)S(1)} %get-tuple-element.12), channel_id=1, source_target_pairs={{0,32},{1,33},{2,34},{3,35},{4,36},{5,37},{6,38},{7,39},{8,40},{9,... | collective-permute-start | bytes 1572872 | tf_op jit(solution)/shard_map/ppermute | solution.py:186
  39.2 16.1 %collective-permute-start.6 = (f32[9,16,8,128]{3,2,1,0:T(8,128)S(1)}, f32[9,16,8,128]{3,2,1,0:T(8,128)S(1)}, u32[]{:S(2)}, u32[]{:S(2)}) collective-permute-start(f32[9,16,8,128]{3,2,1,0:T(8,128)S(1)} %add.21), channel_id=1, source_target_pairs={{0,64},{1,65},{2,66},{3,67},{4,68},{5,69},{6,70},{7,71},{8,72},{9,... | collective-permute-start | bytes 1769480 | tf_op jit(solution)/shard_map/ppermute | solution.py:186
  42.0 24.6 %collective-permute-start.1 = (f32[8,16,8,128]{3,2,1,0:T(8,128)S(1)}, f32[8,16,8,128]{3,2,1,0:T(8,128)S(1)}, u32[]{:S(2)}, u32[]{:S(2)}) collective-permute-start(f32[8,16,8,128]{3,2,1,0:T(8,128)S(1)} %add.19), channel_id=1, source_target_pairs={{0,64},{1,65},{2,66},{3,67},{4,68},{5,69},{6,70},{7,71},{8,72},{9,... | collective-permute-start | bytes 1572872 | tf_op jit(solution)/shard_map/ppermute | solution.py:186
  55.4 14.1 %collective-permute-start.7 = (f32[9,16,8,128]{3,2,1,0:T(8,128)S(1)}, f32[9,16,8,128]{3,2,1,0:T(8,128)S(1)}, u32[]{:S(2)}, u32[]{:S(2)}) collective-permute-start(f32[9,16,8,128]{3,2,1,0:T(8,128)S(1)} %add.22.out_own), channel_id=1, source_target_pairs={{0,32},{1,33},{2,34},{3,35},{4,36},{5,37},{6,38},{7,39},{8,40},{9,... | collective-permute-start | bytes 1769480 | tf_op jit(solution)/shard_map/ppermute | solution.py:186
  66.7 2.8 %collective-permute-start.2 = (f32[8,16,8,128]{3,2,1,0:T(8,128)S(1)}, f32[8,16,8,128]{3,2,1,0:T(8,128)S(1)}, u32[]{:S(2)}, u32[]{:S(2)}) collective-permute-start(f32[8,16,8,128]{3,2,1,0:T(8,128)S(1)} %add.20.mid_own), channel_id=1, source_target_pairs={{0,32},{1,33},{2,34},{3,35},{4,36},{5,37},{6,38},{7,39},{8,40},{9,... | collective-permute-start | bytes 1572872 | tf_op jit(solution)/shard_map/ppermute | solution.py:186
where the time goes:
time: 72.7 us; the launch traced here: 72.5 us
  waiting for transfers between devices  33.2 us (46%)
  Pallas kernels  17.7 us (24%)
  starting transfers between devices  16.6 us (23%)
  local copies, waits for them, and re-layouts  4.03 us (6%)
  between operations  0.74 us (1%)
    ppermute x6, waiting for transfers between devices, send(): return lax.ppermute(x, ('grid', 'tile'), pairs)  24.9 us
    ppermute x6, starting transfers between devices, send(): return lax.ppermute(x, ('grid', 'tile'), pairs)  8.76 us
    ppermute x1, waiting for transfers between devices, on_device(): lax.ppermute(u[12:], 'tile', [(i, (i + 1) % tiles) for i in range(tiles)])  8.32 us
    ppermute x1, starting transfers between devices, on_device(): lax.ppermute(u[:5], 'tile', [((i + 1) % tiles, i) for i in range(tiles)])  7.79 us
    pallas_call x1, Pallas kernels, on_device(): call(middle_kernel, 'middle', 2, 1, (shape(8, HALF, 8, 128), shape(8, HAL...  7.79 us
    pallas_call x1, Pallas kernels, on_device(): call(outer_kernel, 'outer', 2, 5, (shape(9, HALF, 8, 128), shape(9, HALF,...  6.83 us
    pallas_call x1, Pallas kernels, on_device(): call(rebuild_kernel, 'rebuild', 1, 4, shape(16, ROWS, 8, 128), [pltpu.VME...  3.03 us
    slice x1, local copies, waits for them, and re-layouts, on_device(): u[:5]  2.15 us
  transfers between devices with their start and end apart: 8, of which 5 were waited for; matrix products, arithmetic and copies ran while one was open for 3% of the time, Pallas kernels for 11%

commit v1 on v0

v1 whole, which is shorter than its diff:
```python
import functools

import jax
import jax.numpy as jnp
from jax import lax
from jax.experimental import pallas as pl
from jax.experimental.pallas import tpu as pltpu
from jax.sharding import PartitionSpec as P

SCALE = 6.4
ROWS = 32
HALF = ROWS // 2


def devices_of(mesh):
    return mesh.shape["grid"], mesh.shape["tile"]


def layer_update(src, layer, coef, masks, own, other, emit):
    vs, fs, gs = src
    low, ahead, behind = masks
    centre, rate = coef
    for d2 in range(2):
        base = own + d2 * 8
        above = own + 8 if d2 == 0 else other
        below = other + 8 if d2 == 0 else own
        f = [fs[layer, base + k] for k in range(8)]
        g = [gs[layer, base + k] for k in range(8)]
        for k in range(8):
            total = centre * vs[layer, base + k]
            total += rate[0] * (fs[layer + 1, base + k] + gs[layer - 1, base + k])
            total += rate[1] * (fs[layer, above + k] + gs[layer, below + k])
            total += rate[2] * (f[(k + 2) % 8] + g[(k + 6) % 8])
            pair = k ^ 1
            total += rate[3] * jnp.where(
                low, pltpu.roll(f[k] + g[pair], 4, 0), pltpu.roll(f[pair] + g[k], 4, 0)
            )
            total += rate[4] * (
                jnp.take_along_axis(f[k], ahead, axis=0, mode="promise_in_bounds")
                + jnp.take_along_axis(g[k], behind, axis=0, mode="promise_in_bounds")
            )
            total += rate[5] * (pltpu.roll(f[k], 127, 1) + pltpu.roll(g[k], 1, 1))
            emit(d2 * 8 + k, base + k, total)


def lane_masks():
    sub = lax.broadcasted_iota(jnp.int32, (8, 128), 0)
    group = sub - sub % 4
    return sub < 4, group + (sub + 1) % 4, group + (sub + 3) % 4


def coefficients(levels):
    rate = [0.08 / 16.0 * jnp.left_shift(jnp.int32(1), levels[0, d]).astype(jnp.float32) for d in range(6)]
    total = rate[0] + rate[1] + rate[2] + rate[3] + rate[4] + rate[5]
    return 1.0 - 2.0 * total, rate


def put(dst, layer, row, v):
    vs, fs, gs = dst
    q = v * v
    vs[layer, row] = v
    fs[layer, row] = v - q
    gs[layer, row] = v + q


def load_layer(dst, layer, source, index, scale):
    for row in range(ROWS):
        v = source[index, row]
        put(dst, layer, row, v * scale if scale is not None else v)


def step_layer(src, dst, layer, coef, masks):
    for half in range(2):
        layer_update(
            src, layer, coef, masks, half * HALF, (1 - half) * HALF,
            lambda at, row, v: put(dst, layer, row, v),
        )


def last_layer(src, layer, coef, masks, core, sign, keep, send, out):
    for part, ref in ((0, keep), (1, send)):
        own = (core ^ part) * HALF

        def emit(at, row, v, ref=ref):
            ref[out, at] = v * sign

        layer_update(src, layer, coef, masks, own, HALF - own, emit)


def loop(low, high, body):
    def two(i, carry):
        body(low + 2 * i)
        body(low + 2 * i + 1)
        return carry

    lax.fori_loop(0, (high - low) // 2, two, 0)
    if (high - low) % 2:
        body(high - 1)


def middle_kernel(levels, signs, core_ref, u, keep_a, send_a, keep_b, send_b, edge_l, edge_r, *scratch):
    bufs = scratch[:3], scratch[3:]
    coef, masks = coefficients(levels), lane_masks()
    loop(0, 16, lambda i: load_layer(bufs[0], i, u, i, 1.0 / SCALE))
    for step in range(1, 4):
        src, dst = bufs[(step - 1) % 2], bufs[step % 2]
        loop(step, 16 - step, lambda i, s=src, d=dst: step_layer(s, d, i, coef, masks))
        for k in range(2):
            edge_l[2 * (step - 1) + k] = dst[0][step + k]
            edge_r[2 * (step - 1) + k] = dst[0][14 - step + k]
    core, sign = core_ref[0], (signs[0] * 2 - 1).astype(jnp.float32) * SCALE
    loop(0, 4, lambda i: last_layer(bufs[1], i + 4, coef, masks, core, sign, keep_a, send_a, i))
    loop(0, 4, lambda i: last_layer(bufs[1], i + 8, coef, masks, core, sign, keep_b, send_b, i))


def outer_kernel(levels, signs, core_ref, u, left, right, edge_l, edge_r, keep_l, send_l, keep_r, send_r, *scratch):
    bufs = scratch[:3], scratch[3:]
    coef, masks = coefficients(levels), lane_masks()
    for at, source, first, count, scale in (
        (0, left, 0, 4, None), (4, u, 0, 2, 1.0 / SCALE), (13, u, 14, 2, 1.0 / SCALE), (15, right, 0, 4, None)
    ):
        loop(
            0, count,
            lambda i, at=at, source=source, first=first, scale=scale: load_layer(bufs[0], at + i, source, first + i, scale),
        )
    for step in range(1, 4):
        src, dst = bufs[(step - 1) % 2], bufs[step % 2]
        loop(step, step + 4, lambda i, s=src, d=dst: step_layer(s, d, i, coef, masks))
        loop(15 - step, 19 - step, lambda i, s=src, d=dst: step_layer(s, d, i, coef, masks))
        for k in range(2):
            load_layer(dst, 4 + step + k, edge_l, 2 * (step - 1) + k, None)
            load_layer(dst, 13 - step + k, edge_r, 2 * (step - 1) + k, None)
    core, sign = core_ref[0], (signs[0] * 2 - 1).astype(jnp.float32) * SCALE
    loop(0, 4, lambda i: last_layer(bufs[1], i + 4, coef, masks, core, sign, keep_l, send_l, i))
    loop(0, 4, lambda i: last_layer(bufs[1], i + 11, coef, masks, core, sign, keep_r, send_r, i))


def interpolate(levels, points, first, read, write):
    for level in range(1, 5):

        @pl.when(levels[0, 0] == level)
        def _(space=1 << (4 - level)):
            for row in range(first, first + GROUP):
                kept = {}

                def keep(p, row=row, kept=kept):
                    if p not in kept:
                        kept[p] = read(p, row)
                    return kept[p]

                for p in points:
                    anchor, share = p // space * space, p % space / space
                    v = keep(anchor)
                    if share:
                        v = v * (1.0 - share) + keep(anchor + space) * share
                    write(p, row, v)


GROUP = 4


def early_kernel(levels, core_ref, own_l, own_m, other_l, other_m, result, rows, sems):
    copies = []
    for part, (l, m) in enumerate(((own_l, own_m), (other_l, other_m))):
        for first in range(0, HALF, GROUP):

            def write(p, row, v, part=part):
                rows[part, p, row] = v

            interpolate(levels, range(8), first, lambda p, row, l=l, m=m: l[p, row] if p < 4 else m[p - 4, row], write)
            copies.append(pltpu.make_async_copy(
                rows.at[part, :, pl.ds(first, GROUP)],
                result.at[pl.ds(0, 8), pl.ds((core_ref[0] ^ part) * HALF + first, GROUP)],
                sems.at[len(copies)],
            ))
            copies[-1].start()
    for copy in copies:
        copy.wait()


def late_kernel(which, levels, core_ref, m, r, _, result, rows, sems):
    copies = []

    def write(p, row, v):
        rows[p - 8, row] = v

    for first in range(0, HALF, GROUP):
        interpolate(levels, range(8, 16), first, lambda p, row: m[p - 4, row] if p < 12 else r[p - 12, row], write)
        copies.append(pltpu.make_async_copy(
            rows.at[:, pl.ds(first, GROUP)],
            result.at[pl.ds(8, 8), pl.ds((core_ref[0] ^ which) * HALF + first, GROUP)],
            sems.at[len(copies)],
        ))
        copies[-1].start()
    for copy in copies:
        copy.wait()


VMEM = pl.BlockSpec(memory_space=pltpu.VMEM)
ANY = pl.BlockSpec(memory_space=pl.ANY)
SMEM = pl.BlockSpec(memory_space=pltpu.SMEM)
F32 = jnp.float32


def shape(*dims):
    return jax.ShapeDtypeStruct(dims, F32)


def call(kernel, name, specs, out_specs, outs, scratch, cost_us, aliases={}, vmem=24):
    return pl.pallas_call(
        kernel,
        name=name,
        out_shape=outs,
        in_specs=specs,
        out_specs=out_specs,
        scratch_shapes=scratch,
        input_output_aliases=aliases,
        cost_estimate=pl.CostEstimate(flops=0, bytes_accessed=int(cost_us * 3.69e6), transcendentals=0),
        compiler_params=pltpu.CompilerParams(vmem_limit_bytes=vmem << 20),
    )


def on_device(grids, tiles, state_field, levels, sign_bits):
    u = state_field.reshape(16, ROWS, 8, 128)

    def flat(y, core, rest):
        return ((y // 2) * 2 + core) * tiles + (y % 2) * (tiles // 2) + rest

    every = [(y, c, r) for y in range(grids) for c in range(2) for r in range(tiles // 2)]
    to_core = [(flat(y, c, r), flat(y, 1 - c, r)) for y, c, r in every]
    to_far = [(flat(y, c, r), flat((y + 2) % 4, c, r)) for y, c, r in every]

    def send(x, pairs):
        return lax.ppermute(x, ("grid", "tile"), pairs)

    tail, head = u[12:] * (1.0 / SCALE), u[:4] * (1.0 / SCALE)
    up = [(i, (i + 1) % tiles) for i in range(tiles)]
    down = [((i + 1) % tiles, i) for i in range(tiles)]
    left, right = lax.ppermute(tail, "tile", up), lax.ppermute(head, "tile", down)

    core = (lax.axis_index("grid") & 1).astype(jnp.int32).reshape(1)

    def buffers(n):
        return [pltpu.VMEM((n, ROWS, 8, 128), F32)] * 6

    half, edge = shape(4, HALF, 8, 128), shape(6, ROWS, 8, 128)
    keep_a, send_a, keep_b, send_b, edge_l, edge_r = call(
        middle_kernel, "middle", [SMEM] * 3 + [VMEM], (VMEM,) * 6, (half,) * 4 + (edge,) * 2, buffers(16), 6, vmem=16,
    )(levels, sign_bits, core, u)
    got_a, got_b = send(send_a, to_core), send(send_b, to_core)
    got_a, got_b, left, right = lax.optimization_barrier((got_a, got_b, left, right))
    part_m = jnp.concatenate([keep_a + got_a, keep_b + got_b])
    part_m, left, right = lax.optimization_barrier((part_m, left, right))
    far_m = send(part_m, to_far)
    keep_l, send_l, keep_r, send_r = call(
        outer_kernel, "outer", [SMEM] * 3 + [VMEM] * 5, (VMEM,) * 4, (half,) * 4, buffers(19), 6, vmem=20,
    )(levels, sign_bits, core, u, left, right, edge_l, edge_r)
    part_l, part_r = keep_l + send(send_l, to_core), keep_r + send(send_r, to_core)
    far_l = send(part_l, to_far)
    part_r, far_m = lax.optimization_barrier((part_r, far_m))
    far_r = send(part_r, to_far)
    own_l = part_l + far_l
    following = lax.ppermute(own_l[:1], "tile", down)
    other_l = send(own_l, to_core)
    own_m = part_m + far_m
    other_m = send(own_m, to_core)
    whole = shape(16, ROWS, 8, 128)
    result = call(
        early_kernel, "early", [SMEM] * 2 + [VMEM] * 4, ANY, whole,
        [pltpu.VMEM((2, 8, HALF, 8, 128), F32), pltpu.SemaphoreType.DMA((2 * HALF // GROUP,))], 1.5, vmem=8,
    )(levels, core, own_l, own_m, other_l, other_m)
    own_r = jnp.concatenate([part_r + far_r, following])
    own_r, result = lax.optimization_barrier((own_r, result))
    other_r = send(own_r, to_core)
    for which, m, r in ((0, own_m, own_r), (1, other_m, other_r)):
        result = call(
            functools.partial(late_kernel, which), ("late_own", "late_other")[which], [SMEM] * 2 + [VMEM] * 2 + [ANY],
            ANY, whole, [pltpu.VMEM((8, HALF, 8, 128), F32), pltpu.SemaphoreType.DMA((HALF // GROUP,))], 1, {4: 0}, vmem=8,
        )(levels, core, m, r, result)
    return result.reshape(state_field.shape)


def solution(mesh):
    grids, tiles = devices_of(mesh)
    placed = (P("grid", "tile", None, None, None, None, None), P("grid", None), P("grid"))
    return jax.shard_map(
        lambda *args: on_device(grids, tiles, *args),
        mesh=mesh,
        in_specs=placed,
        out_specs=P("grid", "tile", None, None, None, None, None),
        check_vma=False,
    )
```

time: 72.7 us -> 56.6 us (0.78)
  waiting for transfers between devices: 33.2 us -> 8.56 us
  starting transfers between devices: 16.6 us -> 27.7 us
  local copies, waits for them, and re-layouts: 4.03 us -> 0.01 us
  other arithmetic: 0.37 us -> 3.04 us
  Pallas kernels: 17.7 us -> 16.4 us
    ppermute x6 -> x10, waiting for transfers between devices: 24.9 us -> 5.35 us  [send(): return lax.ppermute(x, ('grid', 'tile'), pairs)]
    ppermute x6 -> x10, starting transfers between devices: 8.76 us -> 14.5 us  [send(): return lax.ppermute(x, ('grid', 'tile'), pairs)]
    ppermute x2 -> x3, starting transfers between devices: 7.8 us -> 13.2 us  [the longest x1 5.42 us: on_device(): following = lax.ppermute(own_l[:1], 'tile', down)]
    ppermute x2 -> x3, waiting for transfers between devices: 8.32 us -> 3.21 us  [the longest x1 1.92 us: on_device(): lax.ppermute(tail, 'tile', up)]
    slice x2 -> x1, local copies, waits for them, and re-layouts: 4.02 us -> 0.01 us  [on_device(): following = lax.ppermute(own_l[:1], 'tile', down)]
    mul x0 -> x1, other arithmetic: none -> 2.73 us  [on_device(): tail, head = (u[12:] * (1.0 / SCALE), u[:4] * (1.0 / SCALE))]
    pallas_call x3 -> x5, Pallas kernels: 17.7 us -> 16.4 us  [the longest x1 6.69 us: on_device(): call(middle_kernel, 'middle', [SMEM] * 3 + [VMEM], (VMEM,) * 6, (half,) *...]
  transfers between devices with their start and end apart: 8 -> 13, of which waited for: 5 -> 7; matrix products, arithmetic and copies ran while one was open for 3% -> 0% of each run, Pallas kernels for 11% -> 24%
where the time goes in v1:
time: 56.6 us; the launch traced here: 56.5 us
  starting transfers between devices  27.7 us (49%)
  Pallas kernels  16.4 us (29%)
  waiting for transfers between devices  8.56 us (15%)
  other arithmetic  3.04 us (5%)
  between operations  0.77 us (1%)
    ppermute x10, starting transfers between devices, send(): return lax.ppermute(x, ('grid', 'tile'), pairs)  14.5 us
    pallas_call x1, Pallas kernels, on_device(): call(middle_kernel, 'middle', [SMEM] * 3 + [VMEM], (VMEM,) * 6, (half,) *...  6.69 us
    ppermute x1, starting transfers between devices, on_device(): following = lax.ppermute(own_l[:1], 'tile', down)  5.42 us
    ppermute x10, waiting for transfers between devices, send(): return lax.ppermute(x, ('grid', 'tile'), pairs)  5.35 us
    ppermute x1, starting transfers between devices, on_device(): lax.ppermute(head, 'tile', down)  5.33 us
    pallas_call x1, Pallas kernels, on_device(): call(outer_kernel, 'outer', [SMEM] * 3 + [VMEM] * 5, (VMEM,) * 4, (half,)...  5.31 us
    pallas_call x2, Pallas kernels, on_device(): call(functools.partial(late_kernel, which), ('late_own', 'late_other')[wh...  2.8 us
    mul x1, other arithmetic, on_device(): tail, head = (u[12:] * (1.0 / SCALE), u[:4] * (1.0 / SCALE))  2.73 us
  transfers between devices with their start and end apart: 13, of which 7 were waited for; matrix products, arithmetic and copies ran while one was open for 0% of the time, Pallas kernels for 24%

profile of v1, /device:TPU:1, one launch (start us, length us, event | category | flops | bytes accessed | tf_op | source)
XLA Modules:
  0.0 56.5 jit_solution(15688893403205377031)
XLA Ops:
  0.0 2.7 %slice_multiply_fusion = (f32[1,4,4,4,4,4,128]{6,5,4,3,2,1,0:T(4,128)}, f32[1,4,4,4,4,4,128]{6,5,4,3,2,1,0:T(4,128)}) fusion(f32[1,16,4,4,4,4,128]{6,5,4,3,2,1,0:T(4,128)} %param.3), kind=kLoop, calls=%fused_computation.1 | loop fusion | flops 262144 | bytes 2097152 | tf_op jit(solution)/shard_map/mul | solution.py:236
  2.7 2.5 %collective-permute-start.2 = (f32[4,32,8,128]{3,2,1,0:T(8,128)}, f32[4,32,8,128]{3,2,1,0:T(8,128)S(1)}, u32[]{:S(2)}, u32[]{:S(2)}) collective-permute-start(f32[4,32,8,128]{3,2,1,0:T(8,128)} %bitcast.2), channel_id=1, source_target_pairs={{0,1},{1,2},{2,3},{3,4},{4,5},{5,6},{6,7},{7,8},{8,9},{9,10},{10,1... | collective-permute-start | bytes 1572872 | tf_op jit(solution)/shard_map/ppermute | solution.py:239
  5.2 5.3 %collective-permute-start.3 = (f32[4,32,8,128]{3,2,1,0:T(8,128)}, f32[4,32,8,128]{3,2,1,0:T(8,128)S(1)}, u32[]{:S(2)}, u32[]{:S(2)}) collective-permute-start(f32[4,32,8,128]{3,2,1,0:T(8,128)} %bitcast.3), channel_id=1, source_target_pairs={{1,0},{2,1},{3,2},{4,3},{5,4},{6,5},{7,6},{8,7},{9,8},{10,9},{11,1... | collective-permute-start | bytes 1572872 | tf_op jit(solution)/shard_map/ppermute | solution.py:239
  11.2 6.7 %middle.1 = (f32[4,16,8,128]{3,2,1,0:T(8,128)S(1)}, f32[4,16,8,128]{3,2,1,0:T(8,128)S(1)}, f32[4,16,8,128]{3,2,1,0:T(8,128)S(1)}, f32[4,16,8,128]{3,2,1,0:T(8,12...) custom-call(s32[1,6]{1,0:T(1,128)S(1)} %copy-done.1, s32[1]{0:T(128)S(6)} %copy.8.signs, ...), custom_call_target="tpu_custom_call" | custom-call | bytes 22140000 | tf_op jit(solution)/shard_map/middle/pallas_call | solution.py:247
  17.9 1.0 %collective-permute-start = (f32[4,16,8,128]{3,2,1,0:T(8,128)S(1)}, f32[4,16,8,128]{3,2,1,0:T(8,128)S(1)}, u32[]{:S(2)}, u32[]{:S(2)}) collective-permute-start(f32[4,16,8,128]{3,2,1,0:T(8,128)S(1)} %get-tuple-element.27), channel_id=1, source_target_pairs={{0,32},{1,33},{2,34},{3,35},{4,36},{5,37},{6,38},{7,39},{8,40},{9,... | collective-permute-start | bytes 786440 | tf_op jit(solution)/shard_map/ppermute | solution.py:234
  18.9 0.1 collective-permute-start.1
  19.0 1.1 %collective-permute-done = f32[4,16,8,128]{3,2,1,0:T(8,128)S(1)} collective-permute-done((f32[4,16,8,128]{3,2,1,0:T(8,128)S(1)}, f32[4,16,8,128]{3,2,1,0:T(8,128)S(1)}, u32[]{:S(2)}, u32[]{:S(2)}) %collective-permute-start) | collective-permute-done | bytes 262176 | tf_op jit(solution)/shard_map/ppermute | solution.py:234
  20.1 0.4 collective-permute-done.1
  20.5 1.9 %collective-permute-done.2.left = f32[4,32,8,128]{3,2,1,0:T(8,128)S(1)} collective-permute-done((f32[4,32,8,128]{3,2,1,0:T(8,128)}, f32[4,32,8,128]{3,2,1,0:T(8,128)S(1)}, u32[]{:S(2)}, u32[]{:S(2)}) %collective-permute-start.2) | collective-permute-done | bytes 524320 | tf_op jit(solution)/shard_map/ppermute | solution.py:239
  22.4 0.0 collective-permute-done.3.right
  22.5 2.7 %collective-permute-start.5 = (f32[8,16,8,128]{3,2,1,0:T(8,128)S(1)}, f32[8,16,8,128]{3,2,1,0:T(8,128)S(1)}, u32[]{:S(2)}, u32[]{:S(2)}) collective-permute-start(f32[8,16,8,128]{3,2,1,0:T(8,128)S(1)} %pad_maximum_fusion), channel_id=1, source_target_pairs={{0,64},{1,65},{2,66},{3,67},{4,68},{5,69},{6,70},{7,71},{8,72},{9,... | collective-permute-start | bytes 1572872 | tf_op jit(solution)/shard_map/ppermute | solution.py:234
  25.2 5.3 %outer.1 = (f32[4,16,8,128]{3,2,1,0:T(8,128)S(1)}, f32[4,16,8,128]{3,2,1,0:T(8,128)S(1)}, f32[4,16,8,128]{3,2,1,0:T(8,128)S(1)}, f32[4,16,8,128]{3,2,1,0:T(8,128)S(1)}) custom-call(s32[1,6]{1,0:T(1,128)S(1)} %copy-done.1, s32[1]{0:T(128)S(6)} %copy.8.signs, s32[1]{0:T(128)} %bitcast.core_ref, f32[16,32,8,128]{3,2,1,0:T(8,128)S(1)} %bitcast.6, ...), custom_call_target="tpu_custom_call" | custom-call | bytes 22140000 | tf_op jit(solution)/shard_map/outer/pallas_call | solution.py:255
  30.5 1.6 %collective-permute-start.8 = (f32[4,16,8,128]{3,2,1,0:T(8,128)S(1)}, f32[4,16,8,128]{3,2,1,0:T(8,128)S(1)}, u32[]{:S(2)}, u32[]{:S(2)}) collective-permute-start(f32[4,16,8,128]{3,2,1,0:T(8,128)S(1)} %get-tuple-element.44), channel_id=1, source_target_pairs={{0,32},{1,33},{2,34},{3,35},{4,36},{5,37},{6,38},{7,39},{8,40},{9,... | collective-permute-start | bytes 786440 | tf_op jit(solution)/shard_map/ppermute | solution.py:234
  32.1 0.1 collective-permute-start.4
  32.2 1.1 %collective-permute-done.8 = f32[4,16,8,128]{3,2,1,0:T(8,128)S(1)} collective-permute-done((f32[4,16,8,128]{3,2,1,0:T(8,128)S(1)}, f32[4,16,8,128]{3,2,1,0:T(8,128)S(1)}, u32[]{:S(2)}, u32[]{:S(2)}) %collective-permute-start.8) | collective-permute-done | bytes 262176 | tf_op jit(solution)/shard_map/ppermute | solution.py:234
  33.3 0.4 collective-permute-start.9
  33.7 0.0 collective-permute-done.4
  33.8 2.5 %collective-permute-done.5 = f32[8,16,8,128]{3,2,1,0:T(8,128)S(1)} collective-permute-done((f32[8,16,8,128]{3,2,1,0:T(8,128)S(1)}, f32[8,16,8,128]{3,2,1,0:T(8,128)S(1)}, u32[]{:S(2)}, u32[]{:S(2)}) %collective-permute-start.5) | collective-permute-done | bytes 524320 | tf_op jit(solution)/shard_map/ppermute | solution.py:234
  36.3 0.1 add.24.own_m.m
  36.3 2.9 %collective-permute-start.6 = (f32[8,16,8,128]{3,2,1,0:T(8,128)S(1)}, f32[8,16,8,128]{3,2,1,0:T(8,128)S(1)}, u32[]{:S(2)}, u32[]{:S(2)}) collective-permute-start(f32[8,16,8,128]{3,2,1,0:T(8,128)S(1)} %add.24.own_m.m), channel_id=1, source_target_pairs={{0,32},{1,33},{2,34},{3,35},{4,36},{5,37},{6,38},{7,39},{8,40},{9,... | collective-permute-start | bytes 1572872 | tf_op jit(solution)/shard_map/ppermute | solution.py:234
  39.2 3.7 %collective-permute-start.7 = (f32[4,16,8,128]{3,2,1,0:T(8,128)S(1)}, f32[4,16,8,128]{3,2,1,0:T(8,128)S(1)}, u32[]{:S(2)}, u32[]{:S(2)}) collective-permute-start(f32[4,16,8,128]{3,2,1,0:T(8,128)S(1)} %add.23), channel_id=1, source_target_pairs={{0,64},{1,65},{2,66},{3,67},{4,68},{5,69},{6,70},{7,71},{8,72},{9,... | collective-permute-start | bytes 786440 | tf_op jit(solution)/shard_map/ppermute | solution.py:234
  43.0 0.3 collective-permute-done.9
  43.3 0.9 %collective-permute-start.11 = (f32[4,16,8,128]{3,2,1,0:T(8,128)S(1)}, f32[4,16,8,128]{3,2,1,0:T(8,128)S(1)}, u32[]{:S(2)}, u32[]{:S(2)}) collective-permute-start(f32[4,16,8,128]{3,2,1,0:T(8,128)S(1)} %add.27.own_l), channel_id=1, source_target_pairs={{0,32},{1,33},{2,34},{3,35},{4,36},{5,37},{6,38},{7,39},{8,40},{9,... | collective-permute-start | bytes 786440 | tf_op jit(solution)/shard_map/ppermute | solution.py:234
  44.2 5.4 %collective-permute-start.10 = (f32[1,16,8,128]{3,2,1,0:T(8,128)S(1)}, f32[1,16,8,128]{3,2,1,0:T(8,128)S(1)}, u32[]{:S(2)}, u32[]{:S(2)}) collective-permute-start(f32[1,16,8,128]{3,2,1,0:T(8,128)S(1)} %slice.14), channel_id=1, source_target_pairs={{1,0},{2,1},{3,2},{4,3},{5,4},{6,5},{7,6},{8,7},{9,8},{10,9},{11,1... | collective-permute-start | bytes 196616 | tf_op jit(solution)/shard_map/ppermute | solution.py:263
  49.6 0.0 collective-permute-done.7
  49.6 1.3 %collective-permute-done.10 = f32[1,16,8,128]{3,2,1,0:T(8,128)S(1)} collective-permute-done((f32[1,16,8,128]{3,2,1,0:T(8,128)S(1)}, f32[1,16,8,128]{3,2,1,0:T(8,128)S(1)}, u32[]{:S(2)}, u32[]{:S(2)}) %collective-permute-start.10) | collective-permute-done | bytes 65568 | tf_op jit(solution)/shard_map/ppermute | solution.py:263
  50.9 0.0 collective-permute-done.11.other_l
  51.0 0.0 collective-permute-done.6.other_m.m
  51.0 1.6 %early.1._ = f32[16,32,8,128]{3,2,1,0:T(8,128)} custom-call(s32[1,6]{1,0:T(1,128)S(1)} %copy-done.1, s32[1]{0:T(128)} %bitcast.core_ref, f32[4,16,8,128]{3,2,1,0:T(8,128)S(1)} %add.27.own_l, f32[8,16,8,128]{3,2,1,0:T(8,128)S(1)} %add.24.own_m.m, f32[4,16,8,128]{3,2,1,0:T(8,128)S(1)} %collective-permute-done.11.other_l, ...), custom_call_target="tpu_custom_call" | custom-call | bytes 5535000 | tf_op jit(solution)/shard_map/early/pallas_call | solution.py:268
  52.6 1.1 %collective-permute-start.12 = (f32[5,16,8,128]{3,2,1,0:T(8,128)S(1)}, f32[5,16,8,128]{3,2,1,0:T(8,128)S(1)}, u32[]{:S(2)}, u32[]{:S(2)}) collective-permute-start(f32[5,16,8,128]{3,2,1,0:T(8,128)S(1)} %pad_maximum_fusion.1.r), channel_id=1, source_target_pairs={{0,32},{1,33},{2,34},{3,35},{4,36},{5,37},{6,38},{7,39},{8,40},{9,... | collective-permute-start | bytes 983048 | tf_op jit(solution)/shard_map/ppermute | solution.py:234
  53.6 1.4 %late_own.1._ = f32[16,32,8,128]{3,2,1,0:T(8,128)} custom-call(s32[1,6]{1,0:T(1,128)S(1)} %copy-done.1, s32[1]{0:T(128)} %bitcast.core_ref, f32[8,16,8,128]{3,2,1,0:T(8,128)S(1)} %add.24.own_m.m, f32[5,16,8,128]{3,2,1,0:T(8,128)S(1)} %pad_maximum_fusion.1.r, f32[16,32,8,128]{3,2,1,0:T(8,128)} %early.1._), custom_call_target="tpu_custom_call", output_to_operand_aliasing={{}: (4, {})} | custom-call | bytes 3690000 | tf_op jit(solution)/shard_map/late_own/pallas_call | solution.py:276
  55.1 1.4 %late_other.1 = f32[16,32,8,128]{3,2,1,0:T(8,128)} custom-call(s32[1,6]{1,0:T(1,128)S(1)} %copy-done.1, s32[1]{0:T(128)} %bitcast.core_ref, f32[8,16,8,128]{3,2,1,0:T(8,128)S(1)} %collective-permute-done.6.other_m.m, f32[5,16,8,128]{3,2,1,0:T(8,128)S(1)} %collective-permute-done.12.r, f32[16,32,8,128]{3,2,1,0:T(8,128)} %late_own.1._), custom_call_target="tpu_custom_call", output_to_operand_aliasing={{}: (4, {})} | custom-call | bytes 3690000 | tf_op jit(solution)/shard_map/late_other/pallas_call | solution.py:276
  (14 shorter events, 0.3 us)
Async XLA Ops:
  0.0 11.2 %copy-start = (f32[1,16,4,4,4,4,128]{6,5,4,3,2,1,0:T(4,128)S(1)}, f32[1,16,4,4,4,4,128]{6,5,4,3,2,1,0:T(4,128)}, u32[]{:S(2)}) copy-start(f32[1,16,4,4,4,4,128]{6,5,4,3,2,1,0:T(4,128)} %param.3) | copy-start | bytes 6291460
  0.0 11.2 %copy-start.1 = (s32[1,6]{1,0:T(1,128)S(1)}, s32[1,6]{1,0:T(1,128)}, u32[]{:S(2)}) copy-start(s32[1,6]{1,0:T(1,128)} %levels.9) | copy-start | bytes 76
  2.7 19.7 %collective-permute-start.2 = (f32[4,32,8,128]{3,2,1,0:T(8,128)}, f32[4,32,8,128]{3,2,1,0:T(8,128)S(1)}, u32[]{:S(2)}, u32[]{:S(2)}) collective-permute-start(f32[4,32,8,128]{3,2,1,0:T(8,128)} %bitcast.2), channel_id=1, source_target_pairs={{0,1},{1,2},{2,3},{3,4},{4,5},{5,6},{6,7},{7,8},{8,9},{9,10},{10,1... | collective-permute-start | bytes 1572872 | tf_op jit(solution)/shard_map/ppermute | solution.py:239
  5.2 17.2 %collective-permute-start.3 = (f32[4,32,8,128]{3,2,1,0:T(8,128)}, f32[4,32,8,128]{3,2,1,0:T(8,128)S(1)}, u32[]{:S(2)}, u32[]{:S(2)}) collective-permute-start(f32[4,32,8,128]{3,2,1,0:T(8,128)} %bitcast.3), channel_id=1, source_target_pairs={{1,0},{2,1},{3,2},{4,3},{5,4},{6,5},{7,6},{8,7},{9,8},{10,9},{11,1... | collective-permute-start | bytes 1572872 | tf_op jit(solution)/shard_map/ppermute | solution.py:239
  17.9 2.2 %collective-permute-start = (f32[4,16,8,128]{3,2,1,0:T(8,128)S(1)}, f32[4,16,8,128]{3,2,1,0:T(8,128)S(1)}, u32[]{:S(2)}, u32[]{:S(2)}) collective-permute-start(f32[4,16,8,128]{3,2,1,0:T(8,128)S(1)} %get-tuple-element.27), channel_id=1, source_target_pairs={{0,32},{1,33},{2,34},{3,35},{4,36},{5,37},{6,38},{7,39},{8,40},{9,... | collective-permute-start | bytes 786440 | tf_op jit(solution)/shard_map/ppermute | solution.py:234
  18.9 1.5 %collective-permute-start.1 = (f32[4,16,8,128]{3,2,1,0:T(8,128)S(1)}, f32[4,16,8,128]{3,2,1,0:T(8,128)S(1)}, u32[]{:S(2)}, u32[]{:S(2)}) collective-permute-start(f32[4,16,8,128]{3,2,1,0:T(8,128)S(1)} %get-tuple-element.28), channel_id=1, source_target_pairs={{0,32},{1,33},{2,34},{3,35},{4,36},{5,37},{6,38},{7,39},{8,40},{9,... | collective-permute-start | bytes 786440 | tf_op jit(solution)/shard_map/ppermute | solution.py:234
  22.5 13.8 %collective-permute-start.5 = (f32[8,16,8,128]{3,2,1,0:T(8,128)S(1)}, f32[8,16,8,128]{3,2,1,0:T(8,128)S(1)}, u32[]{:S(2)}, u32[]{:S(2)}) collective-permute-start(f32[8,16,8,128]{3,2,1,0:T(8,128)S(1)} %pad_maximum_fusion), channel_id=1, source_target_pairs={{0,64},{1,65},{2,66},{3,67},{4,68},{5,69},{6,70},{7,71},{8,72},{9,... | collective-permute-start | bytes 1572872 | tf_op jit(solution)/shard_map/ppermute | solution.py:234
  30.5 2.8 %collective-permute-start.8 = (f32[4,16,8,128]{3,2,1,0:T(8,128)S(1)}, f32[4,16,8,128]{3,2,1,0:T(8,128)S(1)}, u32[]{:S(2)}, u32[]{:S(2)}) collective-permute-start(f32[4,16,8,128]{3,2,1,0:T(8,128)S(1)} %get-tuple-element.44), channel_id=1, source_target_pairs={{0,32},{1,33},{2,34},{3,35},{4,36},{5,37},{6,38},{7,39},{8,40},{9,... | collective-permute-start | bytes 786440 | tf_op jit(solution)/shard_map/ppermute | solution.py:234
  32.1 1.6 %collective-permute-start.4 = (f32[4,16,8,128]{3,2,1,0:T(8,128)S(1)}, f32[4,16,8,128]{3,2,1,0:T(8,128)S(1)}, u32[]{:S(2)}, u32[]{:S(2)}) collective-permute-start(f32[4,16,8,128]{3,2,1,0:T(8,128)S(1)} %get-tuple-element.40), channel_id=1, source_target_pairs={{0,32},{1,33},{2,34},{3,35},{4,36},{5,37},{6,38},{7,39},{8,40},{9,... | collective-permute-start | bytes 786440 | tf_op jit(solution)/shard_map/ppermute | solution.py:234
  33.3 10.0 %collective-permute-start.9 = (f32[4,16,8,128]{3,2,1,0:T(8,128)S(1)}, f32[4,16,8,128]{3,2,1,0:T(8,128)S(1)}, u32[]{:S(2)}, u32[]{:S(2)}) collective-permute-start(f32[4,16,8,128]{3,2,1,0:T(8,128)S(1)} %add.26), channel_id=1, source_target_pairs={{0,64},{1,65},{2,66},{3,67},{4,68},{5,69},{6,70},{7,71},{8,72},{9,... | collective-permute-start | bytes 786440 | tf_op jit(solution)/shard_map/ppermute | solution.py:234
  36.3 14.6 %collective-permute-start.6 = (f32[8,16,8,128]{3,2,1,0:T(8,128)S(1)}, f32[8,16,8,128]{3,2,1,0:T(8,128)S(1)}, u32[]{:S(2)}, u32[]{:S(2)}) collective-permute-start(f32[8,16,8,128]{3,2,1,0:T(8,128)S(1)} %add.24.own_m.m), channel_id=1, source_target_pairs={{0,32},{1,33},{2,34},{3,35},{4,36},{5,37},{6,38},{7,39},{8,40},{9,... | collective-permute-start | bytes 1572872 | tf_op jit(solution)/shard_map/ppermute | solution.py:234
  39.2 10.3 %collective-permute-start.7 = (f32[4,16,8,128]{3,2,1,0:T(8,128)S(1)}, f32[4,16,8,128]{3,2,1,0:T(8,128)S(1)}, u32[]{:S(2)}, u32[]{:S(2)}) collective-permute-start(f32[4,16,8,128]{3,2,1,0:T(8,128)S(1)} %add.23), channel_id=1, source_target_pairs={{0,64},{1,65},{2,66},{3,67},{4,68},{5,69},{6,70},{7,71},{8,72},{9,... | collective-permute-start | bytes 786440 | tf_op jit(solution)/shard_map/ppermute | solution.py:234
  43.3 7.6 %collective-permute-start.11 = (f32[4,16,8,128]{3,2,1,0:T(8,128)S(1)}, f32[4,16,8,128]{3,2,1,0:T(8,128)S(1)}, u32[]{:S(2)}, u32[]{:S(2)}) collective-permute-start(f32[4,16,8,128]{3,2,1,0:T(8,128)S(1)} %add.27.own_l), channel_id=1, source_target_pairs={{0,32},{1,33},{2,34},{3,35},{4,36},{5,37},{6,38},{7,39},{8,40},{9,... | collective-permute-start | bytes 786440 | tf_op jit(solution)/shard_map/ppermute | solution.py:234
  44.2 6.7 %collective-permute-start.10 = (f32[1,16,8,128]{3,2,1,0:T(8,128)S(1)}, f32[1,16,8,128]{3,2,1,0:T(8,128)S(1)}, u32[]{:S(2)}, u32[]{:S(2)}) collective-permute-start(f32[1,16,8,128]{3,2,1,0:T(8,128)S(1)} %slice.14), channel_id=1, source_target_pairs={{1,0},{2,1},{3,2},{4,3},{5,4},{6,5},{7,6},{8,7},{9,8},{10,9},{11,1... | collective-permute-start | bytes 196616 | tf_op jit(solution)/shard_map/ppermute | solution.py:263
  52.6 2.5 %collective-permute-start.12 = (f32[5,16,8,128]{3,2,1,0:T(8,128)S(1)}, f32[5,16,8,128]{3,2,1,0:T(8,128)S(1)}, u32[]{:S(2)}, u32[]{:S(2)}) collective-permute-start(f32[5,16,8,128]{3,2,1,0:T(8,128)S(1)} %pad_maximum_fusion.1.r), channel_id=1, source_target_pairs={{0,32},{1,33},{2,34},{3,35},{4,36},{5,37},{6,38},{7,39},{8,40},{9,... | collective-permute-start | bytes 983048 | tf_op jit(solution)/shard_map/ppermute | solution.py:234

commit v2 on v1

--- a/solution.py
+++ b/solution.py
@@ -109,8 +109,8 @@
             edge_l[2 * (step - 1) + k] = dst[0][step + k]
             edge_r[2 * (step - 1) + k] = dst[0][14 - step + k]
     core, sign = core_ref[0], (signs[0] * 2 - 1).astype(jnp.float32) * SCALE
-    loop(0, 4, lambda i: last_layer(bufs[1], i + 4, coef, masks, core, sign, keep_a, send_a, i))
-    loop(0, 4, lambda i: last_layer(bufs[1], i + 8, coef, masks, core, sign, keep_b, send_b, i))
+    loop(0, 6, lambda i: last_layer(bufs[1], i + 4, coef, masks, core, sign, keep_a, send_a, i))
+    loop(0, 2, lambda i: last_layer(bufs[1], i + 10, coef, masks, core, sign, keep_b, send_b, i))
 
 
 def outer_kernel(levels, signs, core_ref, u, left, right, edge_l, edge_r, keep_l, send_l, keep_r, send_r, *scratch):
@@ -185,7 +185,7 @@
         rows[p - 8, row] = v
 
     for first in range(0, HALF, GROUP):
-        interpolate(levels, range(8, 16), first, lambda p, row: m[p - 4, row] if p < 12 else r[p - 12, row], write)
+        interpolate(levels, range(8, 16), first, lambda p, row: m[p - 4, row] if p < 10 else r[p - 10, row], write)
         copies.append(pltpu.make_async_copy(
             rows.at[:, pl.ds(first, GROUP)],
             result.at[pl.ds(8, 8), pl.ds((core_ref[0] ^ which) * HALF + first, GROUP)],
@@ -245,17 +245,17 @@
 
     half, edge = shape(4, HALF, 8, 128), shape(6, ROWS, 8, 128)
     keep_a, send_a, keep_b, send_b, edge_l, edge_r = call(
-        middle_kernel, "middle", [SMEM] * 3 + [VMEM], (VMEM,) * 6, (half,) * 4 + (edge,) * 2, buffers(16), 6, vmem=16,
+        middle_kernel, "middle", [SMEM] * 3 + [VMEM], (VMEM,) * 6, (shape(6, HALF, 8, 128),) * 2 + (shape(2, HALF, 8, 128),) * 2 + (edge,) * 2, buffers(16), 6, vmem=16,
     )(levels, sign_bits, core, u)
     got_a, got_b = send(send_a, to_core), send(send_b, to_core)
-    got_a, got_b, left, right = lax.optimization_barrier((got_a, got_b, left, right))
-    part_m = jnp.concatenate([keep_a + got_a, keep_b + got_b])
-    part_m, left, right = lax.optimization_barrier((part_m, left, right))
+    part_m, part_b = keep_a + got_a, keep_b + got_b
+    part_m, edge_l, edge_r = lax.optimization_barrier((part_m, edge_l, edge_r))
     far_m = send(part_m, to_far)
     keep_l, send_l, keep_r, send_r = call(
         outer_kernel, "outer", [SMEM] * 3 + [VMEM] * 5, (VMEM,) * 4, (half,) * 4, buffers(19), 6, vmem=20,
     )(levels, sign_bits, core, u, left, right, edge_l, edge_r)
-    part_l, part_r = keep_l + send(send_l, to_core), keep_r + send(send_r, to_core)
+    part_l = keep_l + send(send_l, to_core)
+    part_r = jnp.concatenate([part_b, keep_r + send(send_r, to_core)])
     far_l = send(part_l, to_far)
     part_r, far_m = lax.optimization_barrier((part_r, far_m))
     far_r = send(part_r, to_far)
@@ -269,8 +269,8 @@
         early_kernel, "early", [SMEM] * 2 + [VMEM] * 4, ANY, whole,
         [pltpu.VMEM((2, 8, HALF, 8, 128), F32), pltpu.SemaphoreType.DMA((2 * HALF // GROUP,))], 1.5, vmem=8,
     )(levels, core, own_l, own_m, other_l, other_m)
+    far_r, following, result = lax.optimization_barrier((far_r, following, result))
     own_r = jnp.concatenate([part_r + far_r, following])
-    own_r, result = lax.optimization_barrier((own_r, result))
     other_r = send(own_r, to_core)
     for which, m, r in ((0, own_m, own_r), (1, other_m, other_r)):
         result = call(

time: 56.6 us -> 52.7 us (0.931)
  waiting for transfers between devices: 8.56 us -> 5.25 us
  starting transfers between devices: 27.7 us -> 27.1 us
    ppermute x1, waiting for transfers between devices: 1.92 us -> 0.01 us  [on_device(): lax.ppermute(tail, 'tile', up)]
    ppermute x1, waiting for transfers between devices: 1.29 us -> 0.01 us  [on_device(): following = lax.ppermute(own_l[:1], 'tile', down)]
    ppermute x10, starting transfers between devices: 14.5 us -> 13.5 us  [send(): return lax.ppermute(x, ('grid', 'tile'), pairs)]
  transfers between devices with their start and end apart: 13 -> 13, of which waited for: 7 -> 3; matrix products, arithmetic and copies ran while one was open for 0% -> 0% of each run, Pallas kernels for 24% -> 29%
where the time goes in v2:
time: 52.7 us; the launch traced here: 52.6 us
  starting transfers between devices  27.1 us (51%)
  Pallas kernels  16.4 us (31%)
  waiting for transfers between devices  5.25 us (10%)
  other arithmetic  3.05 us (6%)
  between operations  0.77 us (1%)
    ppermute x10, starting transfers between devices, send(): return lax.ppermute(x, ('grid', 'tile'), pairs)  13.5 us
    pallas_call x1, Pallas kernels, on_device(): call(middle_kernel, 'middle', [SMEM] * 3 + [VMEM], (VMEM,) * 6, (shape(6,...  6.69 us
    ppermute x1, starting transfers between devices, on_device(): following = lax.ppermute(own_l[:1], 'tile', down)  5.73 us
    ppermute x1, starting transfers between devices, on_device(): lax.ppermute(head, 'tile', down)  5.33 us
    pallas_call x1, Pallas kernels, on_device(): call(outer_kernel, 'outer', [SMEM] * 3 + [VMEM] * 5, (VMEM,) * 4, (half,)...  5.32 us
    ppermute x10, waiting for transfers between devices, send(): return lax.ppermute(x, ('grid', 'tile'), pairs)  5.24 us
    pallas_call x2, Pallas kernels, on_device(): call(functools.partial(late_kernel, which), ('late_own', 'late_other')[wh...  2.8 us
    mul x1, other arithmetic, on_device(): tail, head = (u[12:] * (1.0 / SCALE), u[:4] * (1.0 / SCALE))  2.73 us
  transfers between devices with their start and end apart: 13, of which 3 were waited for; matrix products, arithmetic and copies ran while one was open for 0% of the time, Pallas kernels for 29%

profile of v2, /device:TPU:1, one launch (start us, length us, event | category | flops | bytes accessed | tf_op | source)
XLA Modules:
  0.0 52.6 jit_solution(17130249141402395639)
XLA Ops:
  0.0 2.7 %slice_multiply_fusion = (f32[1,4,4,4,4,4,128]{6,5,4,3,2,1,0:T(4,128)}, f32[1,4,4,4,4,4,128]{6,5,4,3,2,1,0:T(4,128)}) fusion(f32[1,16,4,4,4,4,128]{6,5,4,3,2,1,0:T(4,128)} %param.3), kind=kLoop, calls=%fused_computation | loop fusion | flops 262144 | bytes 2097152 | tf_op jit(solution)/shard_map/mul | solution.py:236
  2.7 2.5 %collective-permute-start.2 = (f32[4,32,8,128]{3,2,1,0:T(8,128)}, f32[4,32,8,128]{3,2,1,0:T(8,128)S(1)}, u32[]{:S(2)}, u32[]{:S(2)}) collective-permute-start(f32[4,32,8,128]{3,2,1,0:T(8,128)} %bitcast.2), channel_id=1, source_target_pairs={{0,1},{1,2},{2,3},{3,4},{4,5},{5,6},{6,7},{7,8},{8,9},{9,10},{10,1... | collective-permute-start | bytes 1572872 | tf_op jit(solution)/shard_map/ppermute | solution.py:239
  5.2 5.3 %collective-permute-start.3 = (f32[4,32,8,128]{3,2,1,0:T(8,128)}, f32[4,32,8,128]{3,2,1,0:T(8,128)S(1)}, u32[]{:S(2)}, u32[]{:S(2)}) collective-permute-start(f32[4,32,8,128]{3,2,1,0:T(8,128)} %bitcast.3), channel_id=1, source_target_pairs={{1,0},{2,1},{3,2},{4,3},{5,4},{6,5},{7,6},{8,7},{9,8},{10,9},{11,1... | collective-permute-start | bytes 1572872 | tf_op jit(solution)/shard_map/ppermute | solution.py:239
  11.2 6.7 %middle.1 = (f32[6,16,8,128]{3,2,1,0:T(8,128)S(1)}, f32[6,16,8,128]{3,2,1,0:T(8,128)S(1)}, f32[2,16,8,128]{3,2,1,0:T(8,128)S(1)}, f32[2,16,8,128]{3,2,1,0:T(8,12...) custom-call(s32[1,6]{1,0:T(1,128)S(1)} %copy-done.1, s32[1]{0:T(128)S(6)} %copy.8.signs, ...), custom_call_target="tpu_custom_call" | custom-call | bytes 22140000 | tf_op jit(solution)/shard_map/middle/pallas_call | solution.py:247
  17.9 1.0 %collective-permute-start = (f32[6,16,8,128]{3,2,1,0:T(8,128)S(1)}, f32[6,16,8,128]{3,2,1,0:T(8,128)S(1)}, u32[]{:S(2)}, u32[]{:S(2)}) collective-permute-start(f32[6,16,8,128]{3,2,1,0:T(8,128)S(1)} %get-tuple-element.24), channel_id=1, source_target_pairs={{0,32},{1,33},{2,34},{3,35},{4,36},{5,37},{6,38},{7,39},{8,40},{9,... | collective-permute-start | bytes 1179656 | tf_op jit(solution)/shard_map/ppermute | solution.py:234
  18.9 1.3 %collective-permute-done = f32[6,16,8,128]{3,2,1,0:T(8,128)S(1)} collective-permute-done((f32[6,16,8,128]{3,2,1,0:T(8,128)S(1)}, f32[6,16,8,128]{3,2,1,0:T(8,128)S(1)}, u32[]{:S(2)}, u32[]{:S(2)}) %collective-permute-start) | collective-permute-done | bytes 393248 | tf_op jit(solution)/shard_map/ppermute | solution.py:234
  20.3 2.7 %collective-permute-start.5 = (f32[6,16,8,128]{3,2,1,0:T(8,128)S(1)}, f32[6,16,8,128]{3,2,1,0:T(8,128)S(1)}, u32[]{:S(2)}, u32[]{:S(2)}) collective-permute-start(f32[6,16,8,128]{3,2,1,0:T(8,128)S(1)} %add.21), channel_id=1, source_target_pairs={{0,64},{1,65},{2,66},{3,67},{4,68},{5,69},{6,70},{7,71},{8,72},{9,... | collective-permute-start | bytes 1179656 | tf_op jit(solution)/shard_map/ppermute | solution.py:234
  23.0 0.0 collective-permute-done.2.left
  23.0 0.0 collective-permute-done.3.right
  23.0 5.3 %outer.1 = (f32[4,16,8,128]{3,2,1,0:T(8,128)S(1)}, f32[4,16,8,128]{3,2,1,0:T(8,128)S(1)}, f32[4,16,8,128]{3,2,1,0:T(8,128)S(1)}, f32[4,16,8,128]{3,2,1,0:T(8,128)S(1)}) custom-call(s32[1,6]{1,0:T(1,128)S(1)} %copy-done.1, s32[1]{0:T(128)S(6)} %copy.8.signs, s32[1]{0:T(128)} %bitcast.core_ref, f32[16,32,8,128]{3,2,1,0:T(8,128)S(1)} %bitcast.6, ...), custom_call_target="tpu_custom_call" | custom-call | bytes 22140000 | tf_op jit(solution)/shard_map/outer/pallas_call | solution.py:254
  28.4 0.7 %collective-permute-start.8 = (f32[4,16,8,128]{3,2,1,0:T(8,128)S(1)}, f32[4,16,8,128]{3,2,1,0:T(8,128)S(1)}, u32[]{:S(2)}, u32[]{:S(2)}) collective-permute-start(f32[4,16,8,128]{3,2,1,0:T(8,128)S(1)} %get-tuple-element.37), channel_id=1, source_target_pairs={{0,32},{1,33},{2,34},{3,35},{4,36},{5,37},{6,38},{7,39},{8,40},{9,... | collective-permute-start | bytes 786440 | tf_op jit(solution)/shard_map/ppermute | solution.py:234
  29.1 0.1 collective-permute-start.4
  29.2 0.4 collective-permute-start.1
  29.6 0.7 %collective-permute-done.8 = f32[4,16,8,128]{3,2,1,0:T(8,128)S(1)} collective-permute-done((f32[4,16,8,128]{3,2,1,0:T(8,128)S(1)}, f32[4,16,8,128]{3,2,1,0:T(8,128)S(1)}, u32[]{:S(2)}, u32[]{:S(2)}) %collective-permute-start.8) | collective-permute-done | bytes 262176 | tf_op jit(solution)/shard_map/ppermute | solution.py:234
  30.3 2.7 %collective-permute-start.9 = (f32[4,16,8,128]{3,2,1,0:T(8,128)S(1)}, f32[4,16,8,128]{3,2,1,0:T(8,128)S(1)}, u32[]{:S(2)}, u32[]{:S(2)}) collective-permute-start(f32[4,16,8,128]{3,2,1,0:T(8,128)S(1)} %add.25), channel_id=1, source_target_pairs={{0,64},{1,65},{2,66},{3,67},{4,68},{5,69},{6,70},{7,71},{8,72},{9,... | collective-permute-start | bytes 786440 | tf_op jit(solution)/shard_map/ppermute | solution.py:234
  33.0 0.0 collective-permute-done.1
  33.0 0.0 collective-permute-done.4
  33.1 0.0 collective-permute-done.5
  33.2 0.7 %collective-permute-start.6 = (f32[6,16,8,128]{3,2,1,0:T(8,128)S(1)}, f32[6,16,8,128]{3,2,1,0:T(8,128)S(1)}, u32[]{:S(2)}, u32[]{:S(2)}) collective-permute-start(f32[6,16,8,128]{3,2,1,0:T(8,128)S(1)} %add.24.own_m.m), channel_id=1, source_target_pairs={{0,32},{1,33},{2,34},{3,35},{4,36},{5,37},{6,38},{7,39},{8,40},{9,... | collective-permute-start | bytes 1179656 | tf_op jit(solution)/shard_map/ppermute | solution.py:234
  33.9 2.3 %collective-permute-start.7 = (f32[6,16,8,128]{3,2,1,0:T(8,128)S(1)}, f32[6,16,8,128]{3,2,1,0:T(8,128)S(1)}, u32[]{:S(2)}, u32[]{:S(2)}) collective-permute-start(f32[6,16,8,128]{3,2,1,0:T(8,128)S(1)} %pad_maximum_fusion.1), channel_id=1, source_target_pairs={{0,64},{1,65},{2,66},{3,67},{4,68},{5,69},{6,70},{7,71},{8,72},{9,... | collective-permute-start | bytes 1179656 | tf_op jit(solution)/shard_map/ppermute | solution.py:234
  36.2 3.2 %collective-permute-done.9 = f32[4,16,8,128]{3,2,1,0:T(8,128)S(1)} collective-permute-done((f32[4,16,8,128]{3,2,1,0:T(8,128)S(1)}, f32[4,16,8,128]{3,2,1,0:T(8,128)S(1)}, u32[]{:S(2)}, u32[]{:S(2)}) %collective-permute-start.9) | collective-permute-done | bytes 262176 | tf_op jit(solution)/shard_map/ppermute | solution.py:234
  39.4 2.1 %collective-permute-start.11 = (f32[4,16,8,128]{3,2,1,0:T(8,128)S(1)}, f32[4,16,8,128]{3,2,1,0:T(8,128)S(1)}, u32[]{:S(2)}, u32[]{:S(2)}) collective-permute-start(f32[4,16,8,128]{3,2,1,0:T(8,128)S(1)} %add.26.own_l), channel_id=1, source_target_pairs={{0,32},{1,33},{2,34},{3,35},{4,36},{5,37},{6,38},{7,39},{8,40},{9,... | collective-permute-start | bytes 786440 | tf_op jit(solution)/shard_map/ppermute | solution.py:234
  41.5 5.7 %collective-permute-start.10 = (f32[1,16,8,128]{3,2,1,0:T(8,128)S(1)}, f32[1,16,8,128]{3,2,1,0:T(8,128)S(1)}, u32[]{:S(2)}, u32[]{:S(2)}) collective-permute-start(f32[1,16,8,128]{3,2,1,0:T(8,128)S(1)} %slice.14), channel_id=1, source_target_pairs={{1,0},{2,1},{3,2},{4,3},{5,4},{6,5},{7,6},{8,7},{9,8},{10,9},{11,1... | collective-permute-start | bytes 196616 | tf_op jit(solution)/shard_map/ppermute | solution.py:263
  47.2 0.0 collective-permute-done.6.other_m.m
  47.2 0.0 collective-permute-done.11.other_l
  47.2 1.6 %early.1._ = f32[16,32,8,128]{3,2,1,0:T(8,128)} custom-call(s32[1,6]{1,0:T(1,128)S(1)} %copy-done.1, s32[1]{0:T(128)} %bitcast.core_ref, f32[4,16,8,128]{3,2,1,0:T(8,128)S(1)} %add.26.own_l, f32[6,16,8,128]{3,2,1,0:T(8,128)S(1)} %add.24.own_m.m, f32[4,16,8,128]{3,2,1,0:T(8,128)S(1)} %collective-permute-done.11.other_l, ...), custom_call_target="tpu_custom_call" | custom-call | bytes 5535000 | tf_op jit(solution)/shard_map/early/pallas_call | solution.py:268
  48.9 0.0 collective-permute-done.10
  48.9 0.0 collective-permute-done.7
  49.0 0.7 %collective-permute-start.12 = (f32[7,16,8,128]{3,2,1,0:T(8,128)S(1)}, f32[7,16,8,128]{3,2,1,0:T(8,128)S(1)}, u32[]{:S(2)}, u32[]{:S(2)}) collective-permute-start(f32[7,16,8,128]{3,2,1,0:T(8,128)S(1)} %pad_maximum_fusion.r), channel_id=1, source_target_pairs={{0,32},{1,33},{2,34},{3,35},{4,36},{5,37},{6,38},{7,39},{8,40},{9,... | collective-permute-start | bytes 1376264 | tf_op jit(solution)/shard_map/ppermute | solution.py:234
  49.7 1.4 %late_own.1._ = f32[16,32,8,128]{3,2,1,0:T(8,128)} custom-call(s32[1,6]{1,0:T(1,128)S(1)} %copy-done.1, s32[1]{0:T(128)} %bitcast.core_ref, f32[6,16,8,128]{3,2,1,0:T(8,128)S(1)} %add.24.own_m.m, f32[7,16,8,128]{3,2,1,0:T(8,128)S(1)} %pad_maximum_fusion.r, f32[16,32,8,128]{3,2,1,0:T(8,128)} %early.1._), custom_call_target="tpu_custom_call", output_to_operand_aliasing={{}: (4, {})} | custom-call | bytes 3690000 | tf_op jit(solution)/shard_map/late_own/pallas_call | solution.py:276
  51.1 0.0 collective-permute-done.12.r
  51.2 1.4 %late_other.1 = f32[16,32,8,128]{3,2,1,0:T(8,128)} custom-call(s32[1,6]{1,0:T(1,128)S(1)} %copy-done.1, s32[1]{0:T(128)} %bitcast.core_ref, f32[6,16,8,128]{3,2,1,0:T(8,128)S(1)} %collective-permute-done.6.other_m.m, f32[7,16,8,128]{3,2,1,0:T(8,128)S(1)} %collective-permute-done.12.r, f32[16,32,8,128]{3,2,1,0:T(8,128)} %late_own.1._), custom_call_target="tpu_custom_call", output_to_operand_aliasing={{}: (4, {})} | custom-call | bytes 3690000 | tf_op jit(solution)/shard_map/late_other/pallas_call | solution.py:276
  (14 shorter events, 0.3 us)
Async XLA Ops:
  0.0 11.2 %copy-start = (f32[1,16,4,4,4,4,128]{6,5,4,3,2,1,0:T(4,128)S(1)}, f32[1,16,4,4,4,4,128]{6,5,4,3,2,1,0:T(4,128)}, u32[]{:S(2)}) copy-start(f32[1,16,4,4,4,4,128]{6,5,4,3,2,1,0:T(4,128)} %param.3) | copy-start | bytes 6291460
  0.0 11.2 %copy-start.1 = (s32[1,6]{1,0:T(1,128)S(1)}, s32[1,6]{1,0:T(1,128)}, u32[]{:S(2)}) copy-start(s32[1,6]{1,0:T(1,128)} %levels.9) | copy-start | bytes 76
  2.7 20.3 %collective-permute-start.2 = (f32[4,32,8,128]{3,2,1,0:T(8,128)}, f32[4,32,8,128]{3,2,1,0:T(8,128)S(1)}, u32[]{:S(2)}, u32[]{:S(2)}) collective-permute-start(f32[4,32,8,128]{3,2,1,0:T(8,128)} %bitcast.2), channel_id=1, source_target_pairs={{0,1},{1,2},{2,3},{3,4},{4,5},{5,6},{6,7},{7,8},{8,9},{9,10},{10,1... | collective-permute-start | bytes 1572872 | tf_op jit(solution)/shard_map/ppermute | solution.py:239
  5.2 17.8 %collective-permute-start.3 = (f32[4,32,8,128]{3,2,1,0:T(8,128)}, f32[4,32,8,128]{3,2,1,0:T(8,128)S(1)}, u32[]{:S(2)}, u32[]{:S(2)}) collective-permute-start(f32[4,32,8,128]{3,2,1,0:T(8,128)} %bitcast.3), channel_id=1, source_target_pairs={{1,0},{2,1},{3,2},{4,3},{5,4},{6,5},{7,6},{8,7},{9,8},{10,9},{11,1... | collective-permute-start | bytes 1572872 | tf_op jit(solution)/shard_map/ppermute | solution.py:239
  17.9 2.4 %collective-permute-start = (f32[6,16,8,128]{3,2,1,0:T(8,128)S(1)}, f32[6,16,8,128]{3,2,1,0:T(8,128)S(1)}, u32[]{:S(2)}, u32[]{:S(2)}) collective-permute-start(f32[6,16,8,128]{3,2,1,0:T(8,128)S(1)} %get-tuple-element.24), channel_id=1, source_target_pairs={{0,32},{1,33},{2,34},{3,35},{4,36},{5,37},{6,38},{7,39},{8,40},{9,... | collective-permute-start | bytes 1179656 | tf_op jit(solution)/shard_map/ppermute | solution.py:234
  20.3 12.8 %collective-permute-start.5 = (f32[6,16,8,128]{3,2,1,0:T(8,128)S(1)}, f32[6,16,8,128]{3,2,1,0:T(8,128)S(1)}, u32[]{:S(2)}, u32[]{:S(2)}) collective-permute-start(f32[6,16,8,128]{3,2,1,0:T(8,128)S(1)} %add.21), channel_id=1, source_target_pairs={{0,64},{1,65},{2,66},{3,67},{4,68},{5,69},{6,70},{7,71},{8,72},{9,... | collective-permute-start | bytes 1179656 | tf_op jit(solution)/shard_map/ppermute | solution.py:234
  28.4 1.9 %collective-permute-start.8 = (f32[4,16,8,128]{3,2,1,0:T(8,128)S(1)}, f32[4,16,8,128]{3,2,1,0:T(8,128)S(1)}, u32[]{:S(2)}, u32[]{:S(2)}) collective-permute-start(f32[4,16,8,128]{3,2,1,0:T(8,128)S(1)} %get-tuple-element.37), channel_id=1, source_target_pairs={{0,32},{1,33},{2,34},{3,35},{4,36},{5,37},{6,38},{7,39},{8,40},{9,... | collective-permute-start | bytes 786440 | tf_op jit(solution)/shard_map/ppermute | solution.py:234
  29.1 4.0 %collective-permute-start.4 = (f32[4,16,8,128]{3,2,1,0:T(8,128)S(1)}, f32[4,16,8,128]{3,2,1,0:T(8,128)S(1)}, u32[]{:S(2)}, u32[]{:S(2)}) collective-permute-start(f32[4,16,8,128]{3,2,1,0:T(8,128)S(1)} %get-tuple-element.33), channel_id=1, source_target_pairs={{0,32},{1,33},{2,34},{3,35},{4,36},{5,37},{6,38},{7,39},{8,40},{9,... | collective-permute-start | bytes 786440 | tf_op jit(solution)/shard_map/ppermute | solution.py:234
  29.2 3.8 %collective-permute-start.1 = (f32[2,16,8,128]{3,2,1,0:T(8,128)S(1)}, f32[2,16,8,128]{3,2,1,0:T(8,128)S(1)}, u32[]{:S(2)}, u32[]{:S(2)}) collective-permute-start(f32[2,16,8,128]{3,2,1,0:T(8,128)S(1)} %get-tuple-element.29), channel_id=1, source_target_pairs={{0,32},{1,33},{2,34},{3,35},{4,36},{5,37},{6,38},{7,39},{8,40},{9,... | collective-permute-start | bytes 393224 | tf_op jit(solution)/shard_map/ppermute | solution.py:234
  30.3 9.1 %collective-permute-start.9 = (f32[4,16,8,128]{3,2,1,0:T(8,128)S(1)}, f32[4,16,8,128]{3,2,1,0:T(8,128)S(1)}, u32[]{:S(2)}, u32[]{:S(2)}) collective-permute-start(f32[4,16,8,128]{3,2,1,0:T(8,128)S(1)} %add.25), channel_id=1, source_target_pairs={{0,64},{1,65},{2,66},{3,67},{4,68},{5,69},{6,70},{7,71},{8,72},{9,... | collective-permute-start | bytes 786440 | tf_op jit(solution)/shard_map/ppermute | solution.py:234
  33.2 14.1 %collective-permute-start.6 = (f32[6,16,8,128]{3,2,1,0:T(8,128)S(1)}, f32[6,16,8,128]{3,2,1,0:T(8,128)S(1)}, u32[]{:S(2)}, u32[]{:S(2)}) collective-permute-start(f32[6,16,8,128]{3,2,1,0:T(8,128)S(1)} %add.24.own_m.m), channel_id=1, source_target_pairs={{0,32},{1,33},{2,34},{3,35},{4,36},{5,37},{6,38},{7,39},{8,40},{9,... | collective-permute-start | bytes 1179656 | tf_op jit(solution)/shard_map/ppermute | solution.py:234
  33.9 15.0 %collective-permute-start.7 = (f32[6,16,8,128]{3,2,1,0:T(8,128)S(1)}, f32[6,16,8,128]{3,2,1,0:T(8,128)S(1)}, u32[]{:S(2)}, u32[]{:S(2)}) collective-permute-start(f32[6,16,8,128]{3,2,1,0:T(8,128)S(1)} %pad_maximum_fusion.1), channel_id=1, source_target_pairs={{0,64},{1,65},{2,66},{3,67},{4,68},{5,69},{6,70},{7,71},{8,72},{9,... | collective-permute-start | bytes 1179656 | tf_op jit(solution)/shard_map/ppermute | solution.py:234
  39.4 7.8 %collective-permute-start.11 = (f32[4,16,8,128]{3,2,1,0:T(8,128)S(1)}, f32[4,16,8,128]{3,2,1,0:T(8,128)S(1)}, u32[]{:S(2)}, u32[]{:S(2)}) collective-permute-start(f32[4,16,8,128]{3,2,1,0:T(8,128)S(1)} %add.26.own_l), channel_id=1, source_target_pairs={{0,32},{1,33},{2,34},{3,35},{4,36},{5,37},{6,38},{7,39},{8,40},{9,... | collective-permute-start | bytes 786440 | tf_op jit(solution)/shard_map/ppermute | solution.py:234
  41.5 7.3 %collective-permute-start.10 = (f32[1,16,8,128]{3,2,1,0:T(8,128)S(1)}, f32[1,16,8,128]{3,2,1,0:T(8,128)S(1)}, u32[]{:S(2)}, u32[]{:S(2)}) collective-permute-start(f32[1,16,8,128]{3,2,1,0:T(8,128)S(1)} %slice.14), channel_id=1, source_target_pairs={{1,0},{2,1},{3,2},{4,3},{5,4},{6,5},{7,6},{8,7},{9,8},{10,9},{11,1... | collective-permute-start | bytes 196616 | tf_op jit(solution)/shard_map/ppermute | solution.py:263
  49.0 2.2 %collective-permute-start.12 = (f32[7,16,8,128]{3,2,1,0:T(8,128)S(1)}, f32[7,16,8,128]{3,2,1,0:T(8,128)S(1)}, u32[]{:S(2)}, u32[]{:S(2)}) collective-permute-start(f32[7,16,8,128]{3,2,1,0:T(8,128)S(1)} %pad_maximum_fusion.r), channel_id=1, source_target_pairs={{0,32},{1,33},{2,34},{3,35},{4,36},{5,37},{6,38},{7,39},{8,40},{9,... | collective-permute-start | bytes 1376264 | tf_op jit(solution)/shard_map/ppermute | solution.py:234

commit v3 on v2

--- a/solution.py
+++ b/solution.py
@@ -87,15 +87,15 @@
         layer_update(src, layer, coef, masks, own, HALF - own, emit)
 
 
-def loop(low, high, body):
-    def two(i, carry):
-        body(low + 2 * i)
-        body(low + 2 * i + 1)
+def loop(low, high, body, width=4):
+    def several(i, carry):
+        for j in range(width):
+            body(low + width * i + j)
         return carry
 
-    lax.fori_loop(0, (high - low) // 2, two, 0)
-    if (high - low) % 2:
-        body(high - 1)
+    lax.fori_loop(0, (high - low) // width, several, 0)
+    for i in range(high - (high - low) % width, high):
+        body(i)
 
 
 def middle_kernel(levels, signs, core_ref, u, keep_a, send_a, keep_b, send_b, edge_l, edge_r, *scratch):
@@ -125,14 +125,16 @@
         )
     for step in range(1, 4):
         src, dst = bufs[(step - 1) % 2], bufs[step % 2]
-        loop(step, step + 4, lambda i, s=src, d=dst: step_layer(s, d, i, coef, masks))
-        loop(15 - step, 19 - step, lambda i, s=src, d=dst: step_layer(s, d, i, coef, masks))
+        for i in range(4):
+            step_layer(src, dst, step + i, coef, masks)
+            step_layer(src, dst, 15 - step + i, coef, masks)
         for k in range(2):
             load_layer(dst, 4 + step + k, edge_l, 2 * (step - 1) + k, None)
             load_layer(dst, 13 - step + k, edge_r, 2 * (step - 1) + k, None)
     core, sign = core_ref[0], (signs[0] * 2 - 1).astype(jnp.float32) * SCALE
-    loop(0, 4, lambda i: last_layer(bufs[1], i + 4, coef, masks, core, sign, keep_l, send_l, i))
-    loop(0, 4, lambda i: last_layer(bufs[1], i + 11, coef, masks, core, sign, keep_r, send_r, i))
+    for i in range(4):
+        last_layer(bufs[1], i + 4, coef, masks, core, sign, keep_l, send_l, i)
+        last_layer(bufs[1], i + 11, coef, masks, core, sign, keep_r, send_r, i)
 
 
 def interpolate(levels, points, first, read, write):

time: 52.7 us -> 52.1 us (0.989)
  Pallas kernels: 16.4 us -> 15.7 us
  starting transfers between devices: 27.1 us -> 27.7 us
    pallas_call x1, Pallas kernels: 5.32 us -> 4.75 us  [on_device(): call(outer_kernel, 'outer', [SMEM] * 3 + [VMEM] * 5, (VMEM,) * 4, (half,)...]
    ppermute x10, starting transfers between devices: 13.5 us -> 14.1 us  [send(): return lax.ppermute(x, ('grid', 'tile'), pairs)]
  transfers between devices with their start and end apart: 13 -> 13, of which waited for: 3 -> 3; matrix products, arithmetic and copies ran while one was open for 0% -> 0% of each run, Pallas kernels for 29% -> 28%
where the time goes in v3:
time: 52.1 us; the launch traced here: 52 us
  starting transfers between devices  27.7 us (53%)
  Pallas kernels  15.7 us (30%)
  waiting for transfers between devices  4.75 us (9%)
  other arithmetic  3.05 us (6%)
  between operations  0.78 us (1%)
    ppermute x10, starting transfers between devices, send(): return lax.ppermute(x, ('grid', 'tile'), pairs)  14.1 us
    pallas_call x1, Pallas kernels, on_device(): call(middle_kernel, 'middle', [SMEM] * 3 + [VMEM], (VMEM,) * 6, (shape(6,...  6.55 us
    ppermute x1, starting transfers between devices, on_device(): following = lax.ppermute(own_l[:1], 'tile', down)  5.78 us
    ppermute x1, starting transfers between devices, on_device(): lax.ppermute(head, 'tile', down)  5.33 us
    pallas_call x1, Pallas kernels, on_device(): call(outer_kernel, 'outer', [SMEM] * 3 + [VMEM] * 5, (VMEM,) * 4, (half,)...  4.75 us
    ppermute x10, waiting for transfers between devices, send(): return lax.ppermute(x, ('grid', 'tile'), pairs)  4.74 us
    pallas_call x2, Pallas kernels, on_device(): call(functools.partial(late_kernel, which), ('late_own', 'late_other')[wh...  2.8 us
    mul x1, other arithmetic, on_device(): tail, head = (u[12:] * (1.0 / SCALE), u[:4] * (1.0 / SCALE))  2.73 us
  transfers between devices with their start and end apart: 13, of which 3 were waited for; matrix products, arithmetic and copies ran while one was open for 0% of the time, Pallas kernels for 28%

profile of v3, /device:TPU:1, one launch (start us, length us, event | category | flops | bytes accessed | tf_op | source)
XLA Modules:
  0.0 52.0 jit_solution(8359151877512352428)
XLA Ops:
  0.0 2.7 %slice_multiply_fusion = (f32[1,4,4,4,4,4,128]{6,5,4,3,2,1,0:T(4,128)}, f32[1,4,4,4,4,4,128]{6,5,4,3,2,1,0:T(4,128)}) fusion(f32[1,16,4,4,4,4,128]{6,5,4,3,2,1,0:T(4,128)} %param.3), kind=kLoop, calls=%fused_computation | loop fusion | flops 262144 | bytes 2097152 | tf_op jit(solution)/shard_map/mul | solution.py:238
  2.7 2.5 %collective-permute-start.2 = (f32[4,32,8,128]{3,2,1,0:T(8,128)}, f32[4,32,8,128]{3,2,1,0:T(8,128)S(1)}, u32[]{:S(2)}, u32[]{:S(2)}) collective-permute-start(f32[4,32,8,128]{3,2,1,0:T(8,128)} %bitcast.2), channel_id=1, source_target_pairs={{0,1},{1,2},{2,3},{3,4},{4,5},{5,6},{6,7},{7,8},{8,9},{9,10},{10,1... | collective-permute-start | bytes 1572872 | tf_op jit(solution)/shard_map/ppermute | solution.py:241
  5.2 5.3 %collective-permute-start.3 = (f32[4,32,8,128]{3,2,1,0:T(8,128)}, f32[4,32,8,128]{3,2,1,0:T(8,128)S(1)}, u32[]{:S(2)}, u32[]{:S(2)}) collective-permute-start(f32[4,32,8,128]{3,2,1,0:T(8,128)} %bitcast.3), channel_id=1, source_target_pairs={{1,0},{2,1},{3,2},{4,3},{5,4},{6,5},{7,6},{8,7},{9,8},{10,9},{11,1... | collective-permute-start | bytes 1572872 | tf_op jit(solution)/shard_map/ppermute | solution.py:241
  11.2 6.5 %middle.1 = (f32[6,16,8,128]{3,2,1,0:T(8,128)S(1)}, f32[6,16,8,128]{3,2,1,0:T(8,128)S(1)}, f32[2,16,8,128]{3,2,1,0:T(8,128)S(1)}, f32[2,16,8,128]{3,2,1,0:T(8,12...) custom-call(s32[1,6]{1,0:T(1,128)S(1)} %copy-done.1, s32[1]{0:T(128)S(6)} %copy.8.signs, ...), custom_call_target="tpu_custom_call" | custom-call | bytes 22140000 | tf_op jit(solution)/shard_map/middle/pallas_call | solution.py:249
  17.8 1.0 %collective-permute-start = (f32[6,16,8,128]{3,2,1,0:T(8,128)S(1)}, f32[6,16,8,128]{3,2,1,0:T(8,128)S(1)}, u32[]{:S(2)}, u32[]{:S(2)}) collective-permute-start(f32[6,16,8,128]{3,2,1,0:T(8,128)S(1)} %get-tuple-element.24), channel_id=1, source_target_pairs={{0,32},{1,33},{2,34},{3,35},{4,36},{5,37},{6,38},{7,39},{8,40},{9,... | collective-permute-start | bytes 1179656 | tf_op jit(solution)/shard_map/ppermute | solution.py:236
  18.8 1.3 %collective-permute-done = f32[6,16,8,128]{3,2,1,0:T(8,128)S(1)} collective-permute-done((f32[6,16,8,128]{3,2,1,0:T(8,128)S(1)}, f32[6,16,8,128]{3,2,1,0:T(8,128)S(1)}, u32[]{:S(2)}, u32[]{:S(2)}) %collective-permute-start) | collective-permute-done | bytes 393248 | tf_op jit(solution)/shard_map/ppermute | solution.py:236
  20.2 2.7 %collective-permute-start.5 = (f32[6,16,8,128]{3,2,1,0:T(8,128)S(1)}, f32[6,16,8,128]{3,2,1,0:T(8,128)S(1)}, u32[]{:S(2)}, u32[]{:S(2)}) collective-permute-start(f32[6,16,8,128]{3,2,1,0:T(8,128)S(1)} %add.21), channel_id=1, source_target_pairs={{0,64},{1,65},{2,66},{3,67},{4,68},{5,69},{6,70},{7,71},{8,72},{9,... | collective-permute-start | bytes 1179656 | tf_op jit(solution)/shard_map/ppermute | solution.py:236
  22.9 0.0 collective-permute-done.2.left
  22.9 0.0 collective-permute-done.3.right
  22.9 4.7 %outer.1 = (f32[4,16,8,128]{3,2,1,0:T(8,128)S(1)}, f32[4,16,8,128]{3,2,1,0:T(8,128)S(1)}, f32[4,16,8,128]{3,2,1,0:T(8,128)S(1)}, f32[4,16,8,128]{3,2,1,0:T(8,128)S(1)}) custom-call(s32[1,6]{1,0:T(1,128)S(1)} %copy-done.1, s32[1]{0:T(128)S(6)} %copy.8.signs, s32[1]{0:T(128)} %bitcast.core_ref, f32[16,32,8,128]{3,2,1,0:T(8,128)S(1)} %bitcast.6, ...), custom_call_target="tpu_custom_call" | custom-call | bytes 22140000 | tf_op jit(solution)/shard_map/outer/pallas_call | solution.py:256
  27.6 0.8 %collective-permute-start.8 = (f32[4,16,8,128]{3,2,1,0:T(8,128)S(1)}, f32[4,16,8,128]{3,2,1,0:T(8,128)S(1)}, u32[]{:S(2)}, u32[]{:S(2)}) collective-permute-start(f32[4,16,8,128]{3,2,1,0:T(8,128)S(1)} %get-tuple-element.37), channel_id=1, source_target_pairs={{0,32},{1,33},{2,34},{3,35},{4,36},{5,37},{6,38},{7,39},{8,40},{9,... | collective-permute-start | bytes 786440 | tf_op jit(solution)/shard_map/ppermute | solution.py:236
  28.5 0.1 collective-permute-start.4
  28.6 0.4 collective-permute-start.1
  29.0 0.7 %collective-permute-done.8 = f32[4,16,8,128]{3,2,1,0:T(8,128)S(1)} collective-permute-done((f32[4,16,8,128]{3,2,1,0:T(8,128)S(1)}, f32[4,16,8,128]{3,2,1,0:T(8,128)S(1)}, u32[]{:S(2)}, u32[]{:S(2)}) %collective-permute-start.8) | collective-permute-done | bytes 262176 | tf_op jit(solution)/shard_map/ppermute | solution.py:236
  29.7 2.8 %collective-permute-start.9 = (f32[4,16,8,128]{3,2,1,0:T(8,128)S(1)}, f32[4,16,8,128]{3,2,1,0:T(8,128)S(1)}, u32[]{:S(2)}, u32[]{:S(2)}) collective-permute-start(f32[4,16,8,128]{3,2,1,0:T(8,128)S(1)} %add.25), channel_id=1, source_target_pairs={{0,64},{1,65},{2,66},{3,67},{4,68},{5,69},{6,70},{7,71},{8,72},{9,... | collective-permute-start | bytes 786440 | tf_op jit(solution)/shard_map/ppermute | solution.py:236
  32.4 0.0 collective-permute-done.1
  32.5 0.0 collective-permute-done.4
  32.6 0.0 collective-permute-done.5
  32.6 0.8 %collective-permute-start.6 = (f32[6,16,8,128]{3,2,1,0:T(8,128)S(1)}, f32[6,16,8,128]{3,2,1,0:T(8,128)S(1)}, u32[]{:S(2)}, u32[]{:S(2)}) collective-permute-start(f32[6,16,8,128]{3,2,1,0:T(8,128)S(1)} %add.24.own_m.m), channel_id=1, source_target_pairs={{0,32},{1,33},{2,34},{3,35},{4,36},{5,37},{6,38},{7,39},{8,40},{9,... | collective-permute-start | bytes 1179656 | tf_op jit(solution)/shard_map/ppermute | solution.py:236
  33.4 2.6 %collective-permute-start.7 = (f32[6,16,8,128]{3,2,1,0:T(8,128)S(1)}, f32[6,16,8,128]{3,2,1,0:T(8,128)S(1)}, u32[]{:S(2)}, u32[]{:S(2)}) collective-permute-start(f32[6,16,8,128]{3,2,1,0:T(8,128)S(1)} %pad_maximum_fusion.1), channel_id=1, source_target_pairs={{0,64},{1,65},{2,66},{3,67},{4,68},{5,69},{6,70},{7,71},{8,72},{9,... | collective-permute-start | bytes 1179656 | tf_op jit(solution)/shard_map/ppermute | solution.py:236
  36.1 2.7 %collective-permute-done.9 = f32[4,16,8,128]{3,2,1,0:T(8,128)S(1)} collective-permute-done((f32[4,16,8,128]{3,2,1,0:T(8,128)S(1)}, f32[4,16,8,128]{3,2,1,0:T(8,128)S(1)}, u32[]{:S(2)}, u32[]{:S(2)}) %collective-permute-start.9) | collective-permute-done | bytes 262176 | tf_op jit(solution)/shard_map/ppermute | solution.py:236
  38.8 2.1 %collective-permute-start.11 = (f32[4,16,8,128]{3,2,1,0:T(8,128)S(1)}, f32[4,16,8,128]{3,2,1,0:T(8,128)S(1)}, u32[]{:S(2)}, u32[]{:S(2)}) collective-permute-start(f32[4,16,8,128]{3,2,1,0:T(8,128)S(1)} %add.26.own_l), channel_id=1, source_target_pairs={{0,32},{1,33},{2,34},{3,35},{4,36},{5,37},{6,38},{7,39},{8,40},{9,... | collective-permute-start | bytes 786440 | tf_op jit(solution)/shard_map/ppermute | solution.py:236
  40.9 5.8 %collective-permute-start.10 = (f32[1,16,8,128]{3,2,1,0:T(8,128)S(1)}, f32[1,16,8,128]{3,2,1,0:T(8,128)S(1)}, u32[]{:S(2)}, u32[]{:S(2)}) collective-permute-start(f32[1,16,8,128]{3,2,1,0:T(8,128)S(1)} %slice.14), channel_id=1, source_target_pairs={{1,0},{2,1},{3,2},{4,3},{5,4},{6,5},{7,6},{8,7},{9,8},{10,9},{11,1... | collective-permute-start | bytes 196616 | tf_op jit(solution)/shard_map/ppermute | solution.py:265
  46.7 0.0 collective-permute-done.6.other_m.m
  46.7 0.0 collective-permute-done.11.other_l
  46.7 1.6 %early.1._ = f32[16,32,8,128]{3,2,1,0:T(8,128)} custom-call(s32[1,6]{1,0:T(1,128)S(1)} %copy-done.1, s32[1]{0:T(128)} %bitcast.core_ref, f32[4,16,8,128]{3,2,1,0:T(8,128)S(1)} %add.26.own_l, f32[6,16,8,128]{3,2,1,0:T(8,128)S(1)} %add.24.own_m.m, f32[4,16,8,128]{3,2,1,0:T(8,128)S(1)} %collective-permute-done.11.other_l, ...), custom_call_target="tpu_custom_call" | custom-call | bytes 5535000 | tf_op jit(solution)/shard_map/early/pallas_call | solution.py:270
  48.3 0.0 collective-permute-done.10
  48.3 0.0 collective-permute-done.7
  48.4 0.7 %collective-permute-start.12 = (f32[7,16,8,128]{3,2,1,0:T(8,128)S(1)}, f32[7,16,8,128]{3,2,1,0:T(8,128)S(1)}, u32[]{:S(2)}, u32[]{:S(2)}) collective-permute-start(f32[7,16,8,128]{3,2,1,0:T(8,128)S(1)} %pad_maximum_fusion.r), channel_id=1, source_target_pairs={{0,32},{1,33},{2,34},{3,35},{4,36},{5,37},{6,38},{7,39},{8,40},{9,... | collective-permute-start | bytes 1376264 | tf_op jit(solution)/shard_map/ppermute | solution.py:236
  49.1 1.4 %late_own.1._ = f32[16,32,8,128]{3,2,1,0:T(8,128)} custom-call(s32[1,6]{1,0:T(1,128)S(1)} %copy-done.1, s32[1]{0:T(128)} %bitcast.core_ref, f32[6,16,8,128]{3,2,1,0:T(8,128)S(1)} %add.24.own_m.m, f32[7,16,8,128]{3,2,1,0:T(8,128)S(1)} %pad_maximum_fusion.r, f32[16,32,8,128]{3,2,1,0:T(8,128)} %early.1._), custom_call_target="tpu_custom_call", output_to_operand_aliasing={{}: (4, {})} | custom-call | bytes 3690000 | tf_op jit(solution)/shard_map/late_own/pallas_call | solution.py:278
  50.6 0.0 collective-permute-done.12.r
  50.6 1.4 %late_other.1 = f32[16,32,8,128]{3,2,1,0:T(8,128)} custom-call(s32[1,6]{1,0:T(1,128)S(1)} %copy-done.1, s32[1]{0:T(128)} %bitcast.core_ref, f32[6,16,8,128]{3,2,1,0:T(8,128)S(1)} %collective-permute-done.6.other_m.m, f32[7,16,8,128]{3,2,1,0:T(8,128)S(1)} %collective-permute-done.12.r, f32[16,32,8,128]{3,2,1,0:T(8,128)} %late_own.1._), custom_call_target="tpu_custom_call", output_to_operand_aliasing={{}: (4, {})} | custom-call | bytes 3690000 | tf_op jit(solution)/shard_map/late_other/pallas_call | solution.py:278
  (14 shorter events, 0.3 us)
Async XLA Ops:
  0.0 11.2 %copy-start = (f32[1,16,4,4,4,4,128]{6,5,4,3,2,1,0:T(4,128)S(1)}, f32[1,16,4,4,4,4,128]{6,5,4,3,2,1,0:T(4,128)}, u32[]{:S(2)}) copy-start(f32[1,16,4,4,4,4,128]{6,5,4,3,2,1,0:T(4,128)} %param.3) | copy-start | bytes 6291460
  0.0 11.2 %copy-start.1 = (s32[1,6]{1,0:T(1,128)S(1)}, s32[1,6]{1,0:T(1,128)}, u32[]{:S(2)}) copy-start(s32[1,6]{1,0:T(1,128)} %levels.9) | copy-start | bytes 76
  2.7 20.2 %collective-permute-start.2 = (f32[4,32,8,128]{3,2,1,0:T(8,128)}, f32[4,32,8,128]{3,2,1,0:T(8,128)S(1)}, u32[]{:S(2)}, u32[]{:S(2)}) collective-permute-start(f32[4,32,8,128]{3,2,1,0:T(8,128)} %bitcast.2), channel_id=1, source_target_pairs={{0,1},{1,2},{2,3},{3,4},{4,5},{5,6},{6,7},{7,8},{8,9},{9,10},{10,1... | collective-permute-start | bytes 1572872 | tf_op jit(solution)/shard_map/ppermute | solution.py:241
  5.2 17.7 %collective-permute-start.3 = (f32[4,32,8,128]{3,2,1,0:T(8,128)}, f32[4,32,8,128]{3,2,1,0:T(8,128)S(1)}, u32[]{:S(2)}, u32[]{:S(2)}) collective-permute-start(f32[4,32,8,128]{3,2,1,0:T(8,128)} %bitcast.3), channel_id=1, source_target_pairs={{1,0},{2,1},{3,2},{4,3},{5,4},{6,5},{7,6},{8,7},{9,8},{10,9},{11,1... | collective-permute-start | bytes 1572872 | tf_op jit(solution)/shard_map/ppermute | solution.py:241
  17.8 2.4 %collective-permute-start = (f32[6,16,8,128]{3,2,1,0:T(8,128)S(1)}, f32[6,16,8,128]{3,2,1,0:T(8,128)S(1)}, u32[]{:S(2)}, u32[]{:S(2)}) collective-permute-start(f32[6,16,8,128]{3,2,1,0:T(8,128)S(1)} %get-tuple-element.24), channel_id=1, source_target_pairs={{0,32},{1,33},{2,34},{3,35},{4,36},{5,37},{6,38},{7,39},{8,40},{9,... | collective-permute-start | bytes 1179656 | tf_op jit(solution)/shard_map/ppermute | solution.py:236
  20.2 12.4 %collective-permute-start.5 = (f32[6,16,8,128]{3,2,1,0:T(8,128)S(1)}, f32[6,16,8,128]{3,2,1,0:T(8,128)S(1)}, u32[]{:S(2)}, u32[]{:S(2)}) collective-permute-start(f32[6,16,8,128]{3,2,1,0:T(8,128)S(1)} %add.21), channel_id=1, source_target_pairs={{0,64},{1,65},{2,66},{3,67},{4,68},{5,69},{6,70},{7,71},{8,72},{9,... | collective-permute-start | bytes 1179656 | tf_op jit(solution)/shard_map/ppermute | solution.py:236
  27.6 2.0 %collective-permute-start.8 = (f32[4,16,8,128]{3,2,1,0:T(8,128)S(1)}, f32[4,16,8,128]{3,2,1,0:T(8,128)S(1)}, u32[]{:S(2)}, u32[]{:S(2)}) collective-permute-start(f32[4,16,8,128]{3,2,1,0:T(8,128)S(1)} %get-tuple-element.37), channel_id=1, source_target_pairs={{0,32},{1,33},{2,34},{3,35},{4,36},{5,37},{6,38},{7,39},{8,40},{9,... | collective-permute-start | bytes 786440 | tf_op jit(solution)/shard_map/ppermute | solution.py:236
  28.5 4.0 %collective-permute-start.4 = (f32[4,16,8,128]{3,2,1,0:T(8,128)S(1)}, f32[4,16,8,128]{3,2,1,0:T(8,128)S(1)}, u32[]{:S(2)}, u32[]{:S(2)}) collective-permute-start(f32[4,16,8,128]{3,2,1,0:T(8,128)S(1)} %get-tuple-element.33), channel_id=1, source_target_pairs={{0,32},{1,33},{2,34},{3,35},{4,36},{5,37},{6,38},{7,39},{8,40},{9,... | collective-permute-start | bytes 786440 | tf_op jit(solution)/shard_map/ppermute | solution.py:236
  28.6 3.9 %collective-permute-start.1 = (f32[2,16,8,128]{3,2,1,0:T(8,128)S(1)}, f32[2,16,8,128]{3,2,1,0:T(8,128)S(1)}, u32[]{:S(2)}, u32[]{:S(2)}) collective-permute-start(f32[2,16,8,128]{3,2,1,0:T(8,128)S(1)} %get-tuple-element.29), channel_id=1, source_target_pairs={{0,32},{1,33},{2,34},{3,35},{4,36},{5,37},{6,38},{7,39},{8,40},{9,... | collective-permute-start | bytes 393224 | tf_op jit(solution)/shard_map/ppermute | solution.py:236
  29.7 9.1 %collective-permute-start.9 = (f32[4,16,8,128]{3,2,1,0:T(8,128)S(1)}, f32[4,16,8,128]{3,2,1,0:T(8,128)S(1)}, u32[]{:S(2)}, u32[]{:S(2)}) collective-permute-start(f32[4,16,8,128]{3,2,1,0:T(8,128)S(1)} %add.25), channel_id=1, source_target_pairs={{0,64},{1,65},{2,66},{3,67},{4,68},{5,69},{6,70},{7,71},{8,72},{9,... | collective-permute-start | bytes 786440 | tf_op jit(solution)/shard_map/ppermute | solution.py:236
  32.6 14.1 %collective-permute-start.6 = (f32[6,16,8,128]{3,2,1,0:T(8,128)S(1)}, f32[6,16,8,128]{3,2,1,0:T(8,128)S(1)}, u32[]{:S(2)}, u32[]{:S(2)}) collective-permute-start(f32[6,16,8,128]{3,2,1,0:T(8,128)S(1)} %add.24.own_m.m), channel_id=1, source_target_pairs={{0,32},{1,33},{2,34},{3,35},{4,36},{5,37},{6,38},{7,39},{8,40},{9,... | collective-permute-start | bytes 1179656 | tf_op jit(solution)/shard_map/ppermute | solution.py:236
  33.4 14.9 %collective-permute-start.7 = (f32[6,16,8,128]{3,2,1,0:T(8,128)S(1)}, f32[6,16,8,128]{3,2,1,0:T(8,128)S(1)}, u32[]{:S(2)}, u32[]{:S(2)}) collective-permute-start(f32[6,16,8,128]{3,2,1,0:T(8,128)S(1)} %pad_maximum_fusion.1), channel_id=1, source_target_pairs={{0,64},{1,65},{2,66},{3,67},{4,68},{5,69},{6,70},{7,71},{8,72},{9,... | collective-permute-start | bytes 1179656 | tf_op jit(solution)/shard_map/ppermute | solution.py:236
  38.8 7.9 %collective-permute-start.11 = (f32[4,16,8,128]{3,2,1,0:T(8,128)S(1)}, f32[4,16,8,128]{3,2,1,0:T(8,128)S(1)}, u32[]{:S(2)}, u32[]{:S(2)}) collective-permute-start(f32[4,16,8,128]{3,2,1,0:T(8,128)S(1)} %add.26.own_l), channel_id=1, source_target_pairs={{0,32},{1,33},{2,34},{3,35},{4,36},{5,37},{6,38},{7,39},{8,40},{9,... | collective-permute-start | bytes 786440 | tf_op jit(solution)/shard_map/ppermute | solution.py:236
  40.9 7.4 %collective-permute-start.10 = (f32[1,16,8,128]{3,2,1,0:T(8,128)S(1)}, f32[1,16,8,128]{3,2,1,0:T(8,128)S(1)}, u32[]{:S(2)}, u32[]{:S(2)}) collective-permute-start(f32[1,16,8,128]{3,2,1,0:T(8,128)S(1)} %slice.14), channel_id=1, source_target_pairs={{1,0},{2,1},{3,2},{4,3},{5,4},{6,5},{7,6},{8,7},{9,8},{10,9},{11,1... | collective-permute-start | bytes 196616 | tf_op jit(solution)/shard_map/ppermute | solution.py:265
  48.4 2.2 %collective-permute-start.12 = (f32[7,16,8,128]{3,2,1,0:T(8,128)S(1)}, f32[7,16,8,128]{3,2,1,0:T(8,128)S(1)}, u32[]{:S(2)}, u32[]{:S(2)}) collective-permute-start(f32[7,16,8,128]{3,2,1,0:T(8,128)S(1)} %pad_maximum_fusion.r), channel_id=1, source_target_pairs={{0,32},{1,33},{2,34},{3,35},{4,36},{5,37},{6,38},{7,39},{8,40},{9,... | collective-permute-start | bytes 1376264 | tf_op jit(solution)/shard_map/ppermute | solution.py:236

commit v4 on v3

--- a/solution.py
+++ b/solution.py
@@ -158,7 +158,7 @@
                     write(p, row, v)
 
 
-GROUP = 4
+GROUP = 8
 
 
 def early_kernel(levels, core_ref, own_l, own_m, other_l, other_m, result, rows, sems):

time: 52.1 us -> 52.1 us (level)
  transfers between devices with their start and end apart: 13 -> 13, of which waited for: 3 -> 3; matrix products, arithmetic and copies ran while one was open for 0% -> 0% of each run, Pallas kernels for 28% -> 27%
where the time goes in v4:
time: 52.1 us; the launch traced here: 52 us
  starting transfers between devices  27.7 us (53%)
  Pallas kernels  15.7 us (30%)
  waiting for transfers between devices  4.75 us (9%)
  other arithmetic  3.05 us (6%)
  between operations  0.78 us (1%)
    ppermute x10, starting transfers between devices, send(): return lax.ppermute(x, ('grid', 'tile'), pairs)  14.1 us
    pallas_call x1, Pallas kernels, on_device(): call(middle_kernel, 'middle', [SMEM] * 3 + [VMEM], (VMEM,) * 6, (shape(6,...  6.55 us
    ppermute x1, starting transfers between devices, on_device(): following = lax.ppermute(own_l[:1], 'tile', down)  5.78 us
    ppermute x1, starting transfers between devices, on_device(): lax.ppermute(head, 'tile', down)  5.33 us
    pallas_call x1, Pallas kernels, on_device(): call(outer_kernel, 'outer', [SMEM] * 3 + [VMEM] * 5, (VMEM,) * 4, (half,)...  4.75 us
    ppermute x10, waiting for transfers between devices, send(): return lax.ppermute(x, ('grid', 'tile'), pairs)  4.74 us
    pallas_call x2, Pallas kernels, on_device(): call(functools.partial(late_kernel, which), ('late_own', 'late_other')[wh...  2.8 us
    mul x1, other arithmetic, on_device(): tail, head = (u[12:] * (1.0 / SCALE), u[:4] * (1.0 / SCALE))  2.73 us
  transfers between devices with their start and end apart: 13, of which 3 were waited for; matrix products, arithmetic and copies ran while one was open for 0% of the time, Pallas kernels for 27%

profile of v4, /device:TPU:1, one launch (start us, length us, event | category | flops | bytes accessed | tf_op | source)
XLA Modules:
  0.0 52.0 jit_solution(9669867234306750229)
XLA Ops:
  0.0 2.7 %slice_multiply_fusion = (f32[1,4,4,4,4,4,128]{6,5,4,3,2,1,0:T(4,128)}, f32[1,4,4,4,4,4,128]{6,5,4,3,2,1,0:T(4,128)}) fusion(f32[1,16,4,4,4,4,128]{6,5,4,3,2,1,0:T(4,128)} %param.3), kind=kLoop, calls=%fused_computation | loop fusion | flops 262144 | bytes 2097152 | tf_op jit(solution)/shard_map/mul | solution.py:238
  2.7 2.5 %collective-permute-start.2 = (f32[4,32,8,128]{3,2,1,0:T(8,128)}, f32[4,32,8,128]{3,2,1,0:T(8,128)S(1)}, u32[]{:S(2)}, u32[]{:S(2)}) collective-permute-start(f32[4,32,8,128]{3,2,1,0:T(8,128)} %bitcast.2), channel_id=1, source_target_pairs={{0,1},{1,2},{2,3},{3,4},{4,5},{5,6},{6,7},{7,8},{8,9},{9,10},{10,1... | collective-permute-start | bytes 1572872 | tf_op jit(solution)/shard_map/ppermute | solution.py:241
  5.2 5.3 %collective-permute-start.3 = (f32[4,32,8,128]{3,2,1,0:T(8,128)}, f32[4,32,8,128]{3,2,1,0:T(8,128)S(1)}, u32[]{:S(2)}, u32[]{:S(2)}) collective-permute-start(f32[4,32,8,128]{3,2,1,0:T(8,128)} %bitcast.3), channel_id=1, source_target_pairs={{1,0},{2,1},{3,2},{4,3},{5,4},{6,5},{7,6},{8,7},{9,8},{10,9},{11,1... | collective-permute-start | bytes 1572872 | tf_op jit(solution)/shard_map/ppermute | solution.py:241
  11.2 6.5 %middle.1 = (f32[6,16,8,128]{3,2,1,0:T(8,128)S(1)}, f32[6,16,8,128]{3,2,1,0:T(8,128)S(1)}, f32[2,16,8,128]{3,2,1,0:T(8,128)S(1)}, f32[2,16,8,128]{3,2,1,0:T(8,12...) custom-call(s32[1,6]{1,0:T(1,128)S(1)} %copy-done.1, s32[1]{0:T(128)S(6)} %copy.8.signs, ...), custom_call_target="tpu_custom_call" | custom-call | bytes 22140000 | tf_op jit(solution)/shard_map/middle/pallas_call | solution.py:249
  17.8 1.0 %collective-permute-start = (f32[6,16,8,128]{3,2,1,0:T(8,128)S(1)}, f32[6,16,8,128]{3,2,1,0:T(8,128)S(1)}, u32[]{:S(2)}, u32[]{:S(2)}) collective-permute-start(f32[6,16,8,128]{3,2,1,0:T(8,128)S(1)} %get-tuple-element.24), channel_id=1, source_target_pairs={{0,32},{1,33},{2,34},{3,35},{4,36},{5,37},{6,38},{7,39},{8,40},{9,... | collective-permute-start | bytes 1179656 | tf_op jit(solution)/shard_map/ppermute | solution.py:236
  18.8 1.3 %collective-permute-done = f32[6,16,8,128]{3,2,1,0:T(8,128)S(1)} collective-permute-done((f32[6,16,8,128]{3,2,1,0:T(8,128)S(1)}, f32[6,16,8,128]{3,2,1,0:T(8,128)S(1)}, u32[]{:S(2)}, u32[]{:S(2)}) %collective-permute-start) | collective-permute-done | bytes 393248 | tf_op jit(solution)/shard_map/ppermute | solution.py:236
  20.2 2.7 %collective-permute-start.5 = (f32[6,16,8,128]{3,2,1,0:T(8,128)S(1)}, f32[6,16,8,128]{3,2,1,0:T(8,128)S(1)}, u32[]{:S(2)}, u32[]{:S(2)}) collective-permute-start(f32[6,16,8,128]{3,2,1,0:T(8,128)S(1)} %add.21), channel_id=1, source_target_pairs={{0,64},{1,65},{2,66},{3,67},{4,68},{5,69},{6,70},{7,71},{8,72},{9,... | collective-permute-start | bytes 1179656 | tf_op jit(solution)/shard_map/ppermute | solution.py:236
  22.9 0.0 collective-permute-done.2.left
  22.9 0.0 collective-permute-done.3.right
  22.9 4.7 %outer.1 = (f32[4,16,8,128]{3,2,1,0:T(8,128)S(1)}, f32[4,16,8,128]{3,2,1,0:T(8,128)S(1)}, f32[4,16,8,128]{3,2,1,0:T(8,128)S(1)}, f32[4,16,8,128]{3,2,1,0:T(8,128)S(1)}) custom-call(s32[1,6]{1,0:T(1,128)S(1)} %copy-done.1, s32[1]{0:T(128)S(6)} %copy.8.signs, s32[1]{0:T(128)} %bitcast.core_ref, f32[16,32,8,128]{3,2,1,0:T(8,128)S(1)} %bitcast.6, ...), custom_call_target="tpu_custom_call" | custom-call | bytes 22140000 | tf_op jit(solution)/shard_map/outer/pallas_call | solution.py:256
  27.6 0.8 %collective-permute-start.8 = (f32[4,16,8,128]{3,2,1,0:T(8,128)S(1)}, f32[4,16,8,128]{3,2,1,0:T(8,128)S(1)}, u32[]{:S(2)}, u32[]{:S(2)}) collective-permute-start(f32[4,16,8,128]{3,2,1,0:T(8,128)S(1)} %get-tuple-element.37), channel_id=1, source_target_pairs={{0,32},{1,33},{2,34},{3,35},{4,36},{5,37},{6,38},{7,39},{8,40},{9,... | collective-permute-start | bytes 786440 | tf_op jit(solution)/shard_map/ppermute | solution.py:236
  28.5 0.1 collective-permute-start.4
  28.6 0.4 collective-permute-start.1
  29.0 0.7 %collective-permute-done.8 = f32[4,16,8,128]{3,2,1,0:T(8,128)S(1)} collective-permute-done((f32[4,16,8,128]{3,2,1,0:T(8,128)S(1)}, f32[4,16,8,128]{3,2,1,0:T(8,128)S(1)}, u32[]{:S(2)}, u32[]{:S(2)}) %collective-permute-start.8) | collective-permute-done | bytes 262176 | tf_op jit(solution)/shard_map/ppermute | solution.py:236
  29.7 2.8 %collective-permute-start.9 = (f32[4,16,8,128]{3,2,1,0:T(8,128)S(1)}, f32[4,16,8,128]{3,2,1,0:T(8,128)S(1)}, u32[]{:S(2)}, u32[]{:S(2)}) collective-permute-start(f32[4,16,8,128]{3,2,1,0:T(8,128)S(1)} %add.25), channel_id=1, source_target_pairs={{0,64},{1,65},{2,66},{3,67},{4,68},{5,69},{6,70},{7,71},{8,72},{9,... | collective-permute-start | bytes 786440 | tf_op jit(solution)/shard_map/ppermute | solution.py:236
  32.4 0.0 collective-permute-done.1
  32.5 0.0 collective-permute-done.4
  32.6 0.0 collective-permute-done.5
  32.6 0.8 %collective-permute-start.6 = (f32[6,16,8,128]{3,2,1,0:T(8,128)S(1)}, f32[6,16,8,128]{3,2,1,0:T(8,128)S(1)}, u32[]{:S(2)}, u32[]{:S(2)}) collective-permute-start(f32[6,16,8,128]{3,2,1,0:T(8,128)S(1)} %add.24.own_m.m), channel_id=1, source_target_pairs={{0,32},{1,33},{2,34},{3,35},{4,36},{5,37},{6,38},{7,39},{8,40},{9,... | collective-permute-start | bytes 1179656 | tf_op jit(solution)/shard_map/ppermute | solution.py:236
  33.4 2.6 %collective-permute-start.7 = (f32[6,16,8,128]{3,2,1,0:T(8,128)S(1)}, f32[6,16,8,128]{3,2,1,0:T(8,128)S(1)}, u32[]{:S(2)}, u32[]{:S(2)}) collective-permute-start(f32[6,16,8,128]{3,2,1,0:T(8,128)S(1)} %pad_maximum_fusion.1), channel_id=1, source_target_pairs={{0,64},{1,65},{2,66},{3,67},{4,68},{5,69},{6,70},{7,71},{8,72},{9,... | collective-permute-start | bytes 1179656 | tf_op jit(solution)/shard_map/ppermute | solution.py:236
  36.1 2.7 %collective-permute-done.9 = f32[4,16,8,128]{3,2,1,0:T(8,128)S(1)} collective-permute-done((f32[4,16,8,128]{3,2,1,0:T(8,128)S(1)}, f32[4,16,8,128]{3,2,1,0:T(8,128)S(1)}, u32[]{:S(2)}, u32[]{:S(2)}) %collective-permute-start.9) | collective-permute-done | bytes 262176 | tf_op jit(solution)/shard_map/ppermute | solution.py:236
  38.8 2.1 %collective-permute-start.11 = (f32[4,16,8,128]{3,2,1,0:T(8,128)S(1)}, f32[4,16,8,128]{3,2,1,0:T(8,128)S(1)}, u32[]{:S(2)}, u32[]{:S(2)}) collective-permute-start(f32[4,16,8,128]{3,2,1,0:T(8,128)S(1)} %add.26.own_l), channel_id=1, source_target_pairs={{0,32},{1,33},{2,34},{3,35},{4,36},{5,37},{6,38},{7,39},{8,40},{9,... | collective-permute-start | bytes 786440 | tf_op jit(solution)/shard_map/ppermute | solution.py:236
  40.9 5.8 %collective-permute-start.10 = (f32[1,16,8,128]{3,2,1,0:T(8,128)S(1)}, f32[1,16,8,128]{3,2,1,0:T(8,128)S(1)}, u32[]{:S(2)}, u32[]{:S(2)}) collective-permute-start(f32[1,16,8,128]{3,2,1,0:T(8,128)S(1)} %slice.14), channel_id=1, source_target_pairs={{1,0},{2,1},{3,2},{4,3},{5,4},{6,5},{7,6},{8,7},{9,8},{10,9},{11,1... | collective-permute-start | bytes 196616 | tf_op jit(solution)/shard_map/ppermute | solution.py:265
  46.7 0.0 collective-permute-done.6.other_m.m
  46.7 0.0 collective-permute-done.11.other_l
  46.7 1.6 %early.1._ = f32[16,32,8,128]{3,2,1,0:T(8,128)} custom-call(s32[1,6]{1,0:T(1,128)S(1)} %copy-done.1, s32[1]{0:T(128)} %bitcast.core_ref, f32[4,16,8,128]{3,2,1,0:T(8,128)S(1)} %add.26.own_l, f32[6,16,8,128]{3,2,1,0:T(8,128)S(1)} %add.24.own_m.m, f32[4,16,8,128]{3,2,1,0:T(8,128)S(1)} %collective-permute-done.11.other_l, ...), custom_call_target="tpu_custom_call" | custom-call | bytes 5535000 | tf_op jit(solution)/shard_map/early/pallas_call | solution.py:270
  48.3 0.0 collective-permute-done.10
  48.3 0.0 collective-permute-done.7
  48.4 0.8 %collective-permute-start.12 = (f32[7,16,8,128]{3,2,1,0:T(8,128)S(1)}, f32[7,16,8,128]{3,2,1,0:T(8,128)S(1)}, u32[]{:S(2)}, u32[]{:S(2)}) collective-permute-start(f32[7,16,8,128]{3,2,1,0:T(8,128)S(1)} %pad_maximum_fusion.r), channel_id=1, source_target_pairs={{0,32},{1,33},{2,34},{3,35},{4,36},{5,37},{6,38},{7,39},{8,40},{9,... | collective-permute-start | bytes 1376264 | tf_op jit(solution)/shard_map/ppermute | solution.py:236
  49.1 1.4 %late_own.1._ = f32[16,32,8,128]{3,2,1,0:T(8,128)} custom-call(s32[1,6]{1,0:T(1,128)S(1)} %copy-done.1, s32[1]{0:T(128)} %bitcast.core_ref, f32[6,16,8,128]{3,2,1,0:T(8,128)S(1)} %add.24.own_m.m, f32[7,16,8,128]{3,2,1,0:T(8,128)S(1)} %pad_maximum_fusion.r, f32[16,32,8,128]{3,2,1,0:T(8,128)} %early.1._), custom_call_target="tpu_custom_call", output_to_operand_aliasing={{}: (4, {})} | custom-call | bytes 3690000 | tf_op jit(solution)/shard_map/late_own/pallas_call | solution.py:278
  50.6 0.0 collective-permute-done.12.r
  50.6 1.4 %late_other.1 = f32[16,32,8,128]{3,2,1,0:T(8,128)} custom-call(s32[1,6]{1,0:T(1,128)S(1)} %copy-done.1, s32[1]{0:T(128)} %bitcast.core_ref, f32[6,16,8,128]{3,2,1,0:T(8,128)S(1)} %collective-permute-done.6.other_m.m, f32[7,16,8,128]{3,2,1,0:T(8,128)S(1)} %collective-permute-done.12.r, f32[16,32,8,128]{3,2,1,0:T(8,128)} %late_own.1._), custom_call_target="tpu_custom_call", output_to_operand_aliasing={{}: (4, {})} | custom-call | bytes 3690000 | tf_op jit(solution)/shard_map/late_other/pallas_call | solution.py:278
  (14 shorter events, 0.3 us)
Async XLA Ops:
  0.0 11.2 %copy-start = (f32[1,16,4,4,4,4,128]{6,5,4,3,2,1,0:T(4,128)S(1)}, f32[1,16,4,4,4,4,128]{6,5,4,3,2,1,0:T(4,128)}, u32[]{:S(2)}) copy-start(f32[1,16,4,4,4,4,128]{6,5,4,3,2,1,0:T(4,128)} %param.3) | copy-start | bytes 6291460
  0.0 11.2 %copy-start.1 = (s32[1,6]{1,0:T(1,128)S(1)}, s32[1,6]{1,0:T(1,128)}, u32[]{:S(2)}) copy-start(s32[1,6]{1,0:T(1,128)} %levels.9) | copy-start | bytes 76
  2.7 20.2 %collective-permute-start.2 = (f32[4,32,8,128]{3,2,1,0:T(8,128)}, f32[4,32,8,128]{3,2,1,0:T(8,128)S(1)}, u32[]{:S(2)}, u32[]{:S(2)}) collective-permute-start(f32[4,32,8,128]{3,2,1,0:T(8,128)} %bitcast.2), channel_id=1, source_target_pairs={{0,1},{1,2},{2,3},{3,4},{4,5},{5,6},{6,7},{7,8},{8,9},{9,10},{10,1... | collective-permute-start | bytes 1572872 | tf_op jit(solution)/shard_map/ppermute | solution.py:241
  5.2 17.7 %collective-permute-start.3 = (f32[4,32,8,128]{3,2,1,0:T(8,128)}, f32[4,32,8,128]{3,2,1,0:T(8,128)S(1)}, u32[]{:S(2)}, u32[]{:S(2)}) collective-permute-start(f32[4,32,8,128]{3,2,1,0:T(8,128)} %bitcast.3), channel_id=1, source_target_pairs={{1,0},{2,1},{3,2},{4,3},{5,4},{6,5},{7,6},{8,7},{9,8},{10,9},{11,1... | collective-permute-start | bytes 1572872 | tf_op jit(solution)/shard_map/ppermute | solution.py:241
  17.8 2.4 %collective-permute-start = (f32[6,16,8,128]{3,2,1,0:T(8,128)S(1)}, f32[6,16,8,128]{3,2,1,0:T(8,128)S(1)}, u32[]{:S(2)}, u32[]{:S(2)}) collective-permute-start(f32[6,16,8,128]{3,2,1,0:T(8,128)S(1)} %get-tuple-element.24), channel_id=1, source_target_pairs={{0,32},{1,33},{2,34},{3,35},{4,36},{5,37},{6,38},{7,39},{8,40},{9,... | collective-permute-start | bytes 1179656 | tf_op jit(solution)/shard_map/ppermute | solution.py:236
  20.2 12.4 %collective-permute-start.5 = (f32[6,16,8,128]{3,2,1,0:T(8,128)S(1)}, f32[6,16,8,128]{3,2,1,0:T(8,128)S(1)}, u32[]{:S(2)}, u32[]{:S(2)}) collective-permute-start(f32[6,16,8,128]{3,2,1,0:T(8,128)S(1)} %add.21), channel_id=1, source_target_pairs={{0,64},{1,65},{2,66},{3,67},{4,68},{5,69},{6,70},{7,71},{8,72},{9,... | collective-permute-start | bytes 1179656 | tf_op jit(solution)/shard_map/ppermute | solution.py:236
  27.6 2.0 %collective-permute-start.8 = (f32[4,16,8,128]{3,2,1,0:T(8,128)S(1)}, f32[4,16,8,128]{3,2,1,0:T(8,128)S(1)}, u32[]{:S(2)}, u32[]{:S(2)}) collective-permute-start(f32[4,16,8,128]{3,2,1,0:T(8,128)S(1)} %get-tuple-element.37), channel_id=1, source_target_pairs={{0,32},{1,33},{2,34},{3,35},{4,36},{5,37},{6,38},{7,39},{8,40},{9,... | collective-permute-start | bytes 786440 | tf_op jit(solution)/shard_map/ppermute | solution.py:236
  28.5 4.0 %collective-permute-start.4 = (f32[4,16,8,128]{3,2,1,0:T(8,128)S(1)}, f32[4,16,8,128]{3,2,1,0:T(8,128)S(1)}, u32[]{:S(2)}, u32[]{:S(2)}) collective-permute-start(f32[4,16,8,128]{3,2,1,0:T(8,128)S(1)} %get-tuple-element.33), channel_id=1, source_target_pairs={{0,32},{1,33},{2,34},{3,35},{4,36},{5,37},{6,38},{7,39},{8,40},{9,... | collective-permute-start | bytes 786440 | tf_op jit(solution)/shard_map/ppermute | solution.py:236
  28.6 3.9 %collective-permute-start.1 = (f32[2,16,8,128]{3,2,1,0:T(8,128)S(1)}, f32[2,16,8,128]{3,2,1,0:T(8,128)S(1)}, u32[]{:S(2)}, u32[]{:S(2)}) collective-permute-start(f32[2,16,8,128]{3,2,1,0:T(8,128)S(1)} %get-tuple-element.29), channel_id=1, source_target_pairs={{0,32},{1,33},{2,34},{3,35},{4,36},{5,37},{6,38},{7,39},{8,40},{9,... | collective-permute-start | bytes 393224 | tf_op jit(solution)/shard_map/ppermute | solution.py:236
  29.7 9.1 %collective-permute-start.9 = (f32[4,16,8,128]{3,2,1,0:T(8,128)S(1)}, f32[4,16,8,128]{3,2,1,0:T(8,128)S(1)}, u32[]{:S(2)}, u32[]{:S(2)}) collective-permute-start(f32[4,16,8,128]{3,2,1,0:T(8,128)S(1)} %add.25), channel_id=1, source_target_pairs={{0,64},{1,65},{2,66},{3,67},{4,68},{5,69},{6,70},{7,71},{8,72},{9,... | collective-permute-start | bytes 786440 | tf_op jit(solution)/shard_map/ppermute | solution.py:236
  32.6 14.1 %collective-permute-start.6 = (f32[6,16,8,128]{3,2,1,0:T(8,128)S(1)}, f32[6,16,8,128]{3,2,1,0:T(8,128)S(1)}, u32[]{:S(2)}, u32[]{:S(2)}) collective-permute-start(f32[6,16,8,128]{3,2,1,0:T(8,128)S(1)} %add.24.own_m.m), channel_id=1, source_target_pairs={{0,32},{1,33},{2,34},{3,35},{4,36},{5,37},{6,38},{7,39},{8,40},{9,... | collective-permute-start | bytes 1179656 | tf_op jit(solution)/shard_map/ppermute | solution.py:236
  33.4 14.9 %collective-permute-start.7 = (f32[6,16,8,128]{3,2,1,0:T(8,128)S(1)}, f32[6,16,8,128]{3,2,1,0:T(8,128)S(1)}, u32[]{:S(2)}, u32[]{:S(2)}) collective-permute-start(f32[6,16,8,128]{3,2,1,0:T(8,128)S(1)} %pad_maximum_fusion.1), channel_id=1, source_target_pairs={{0,64},{1,65},{2,66},{3,67},{4,68},{5,69},{6,70},{7,71},{8,72},{9,... | collective-permute-start | bytes 1179656 | tf_op jit(solution)/shard_map/ppermute | solution.py:236
  38.8 7.9 %collective-permute-start.11 = (f32[4,16,8,128]{3,2,1,0:T(8,128)S(1)}, f32[4,16,8,128]{3,2,1,0:T(8,128)S(1)}, u32[]{:S(2)}, u32[]{:S(2)}) collective-permute-start(f32[4,16,8,128]{3,2,1,0:T(8,128)S(1)} %add.26.own_l), channel_id=1, source_target_pairs={{0,32},{1,33},{2,34},{3,35},{4,36},{5,37},{6,38},{7,39},{8,40},{9,... | collective-permute-start | bytes 786440 | tf_op jit(solution)/shard_map/ppermute | solution.py:236
  40.9 7.4 %collective-permute-start.10 = (f32[1,16,8,128]{3,2,1,0:T(8,128)S(1)}, f32[1,16,8,128]{3,2,1,0:T(8,128)S(1)}, u32[]{:S(2)}, u32[]{:S(2)}) collective-permute-start(f32[1,16,8,128]{3,2,1,0:T(8,128)S(1)} %slice.14), channel_id=1, source_target_pairs={{1,0},{2,1},{3,2},{4,3},{5,4},{6,5},{7,6},{8,7},{9,8},{10,9},{11,1... | collective-permute-start | bytes 196616 | tf_op jit(solution)/shard_map/ppermute | solution.py:265
  48.4 2.2 %collective-permute-start.12 = (f32[7,16,8,128]{3,2,1,0:T(8,128)S(1)}, f32[7,16,8,128]{3,2,1,0:T(8,128)S(1)}, u32[]{:S(2)}, u32[]{:S(2)}) collective-permute-start(f32[7,16,8,128]{3,2,1,0:T(8,128)S(1)} %pad_maximum_fusion.r), channel_id=1, source_target_pairs={{0,32},{1,33},{2,34},{3,35},{4,36},{5,37},{6,38},{7,39},{8,40},{9,... | collective-permute-start | bytes 1376264 | tf_op jit(solution)/shard_map/ppermute | solution.py:236
